TPU v7x, 128 devices: a whole 4x4x4 slice. The times are simulated.
128 devices in a mesh: gx: 16 (over x, z), gy: 8 (over y, core).
Axes of the slice: x: 4, y: 4, z: 4, core: 2. Of those that a mesh axis runs over, the one named last changes fastest.
Arguments:
- factor_grads: bfloat16 [512, 196608], P(('gx', 'gy')), may hold values from -0.29882812 to 0.29882812
- latents: bfloat16 [512, 1024], P(('gx', 'gy')), may hold values from -6 to 6
- task_ids: int32 [512], P(('gx', 'gy')), may hold values from 0 to 511, each once
- offsets: int32 [160], replicated, may hold values from 0 to 196607, as said below
- target_scale: float32 [160], replicated, may hold values from 0.5 to 2
- momentum: float32 [1024, 196608], P(None, ('gx', 'gy')), may hold values from -6 to 6
Outputs:
- new_momentum: float32 [1024, 196608], P(None, ('gx', 'gy'))
- step: float32 [1024, 196608], P(None, ('gx', 'gy'))
Inputs may be any that keep to these rules, and one draw needn't show every extreme that they name: `task_ids`: a permutation of 0 to 511. offsets[0] is 0 and offsets rise strictly.
All inputs are finite; a program needn't handle non-finite values.
Results may differ from a plain program's by a relative error of at most 0.0003.
Values may be sent and summed in bfloat16 or wider, within the bound.
A program may use at most 128 MiB of HBM per device.

v0:
```python
import math

import jax
import jax.numpy as jnp
from jax import lax
from jax.sharding import PartitionSpec as P

OUT = 196608
ITERS = 2


MOMENTUM_DECAY = 0.95
EPSILON = 1e-07
NEWTON_A = 3.4445
NEWTON_B = -4.775
NEWTON_C = 2.0315


def local_gram(matrix):
    return lax.dot_general(
        matrix,
        matrix,
        (((1,), (1,)), ((), ())),
        precision=lax.Precision.HIGHEST,
        preferred_element_type=jnp.float32,
    )


def block_slots():
    slot_of = {}
    for first_block in range(8):
        for second_block in range(first_block, 8):
            slot_of[first_block, second_block] = len(slot_of)
    return slot_of


def unpack_upper(packed):
    slot_of = block_slots()
    band_rows = []
    for first_block in range(8):
        band = []
        for second_block in range(8):
            if second_block >= first_block:
                band.append(packed[slot_of[first_block, second_block]])
            else:
                band.append(packed[slot_of[second_block, first_block]].T)
        band_rows.append(jnp.concatenate(band, axis=1))
    return jnp.concatenate(band_rows, axis=0)


def gram_square(gram_matrix):
    block_size = gram_matrix.shape[0] // 8
    pieces = []
    for first_block in range(8):
        left = gram_matrix[first_block * block_size : (first_block + 1) * block_size, :]
        for second_block in range(first_block, 8):
            right = gram_matrix[:, second_block * block_size : (second_block + 1) * block_size]
            pieces.append(jnp.dot(left, right, precision=lax.Precision.HIGHEST))
    return unpack_upper(jnp.stack(pieces))


def summed_gram(matrix):
    partial_gram = local_gram(matrix)
    return lax.psum(partial_gram, ("gx", "gy"))


def per_device(factor_grads, latents, task_ids, offsets, target_scale, momentum):
    all_latents, all_ids = (
        lax.all_gather(latents, ("gx", "gy"), axis=0, tiled=True),
        lax.all_gather(task_ids, ("gx", "gy"), axis=0, tiled=True),
    )
    columns = lax.all_to_all(factor_grads, ("gx", "gy"), split_axis=1, concat_axis=0, tiled=True)
    task_latent = all_latents[all_ids]
    head_grad = lax.dot_general(
        task_latent, columns, (((0,), (0,)), ((), ())), preferred_element_type=jnp.float32
    )
    new_momentum = MOMENTUM_DECAY * momentum + head_grad
    blended = head_grad + MOMENTUM_DECAY * new_momentum
    squares = lax.psum(jnp.sum(blended * blended), ("gx", "gy"))
    frobenius = jnp.sqrt(squares)
    orthogonal = blended / (frobenius + EPSILON)
    for iteration in range(ITERS):
        gram_matrix = summed_gram(orthogonal)
        poly_matrix = NEWTON_B * gram_matrix + NEWTON_C * gram_square(gram_matrix)
        orthogonal = NEWTON_A * orthogonal + jnp.dot(
            poly_matrix, orthogonal, precision=lax.Precision.HIGHEST
        )
    column_count = orthogonal.shape[1]
    column_index = lax.axis_index(("gx", "gy")) * column_count + jnp.arange(
        column_count, dtype=jnp.int32
    )
    beyond = (column_index[:, None] >= offsets[None, :]).astype(jnp.float32)
    deltas = target_scale - jnp.concatenate([jnp.zeros((1,), jnp.float32), target_scale[:-1]])
    column_scale = jnp.sum(beyond * deltas[None, :], axis=1)
    step = math.sqrt(OUT) * column_scale[None, :] * orthogonal
    return (new_momentum, step)


def solution(mesh):
    placed = (
        P(("gx", "gy"), None),
        P(("gx", "gy"), None),
        P(("gx", "gy")),
        P(),
        P(),
        P(None, ("gx", "gy")),
    )
    return jax.shard_map(
        per_device,
        mesh=mesh,
        in_specs=placed,
        out_specs=(P(None, ("gx", "gy")), P(None, ("gx", "gy"))),
        check_vma=False,
    )
```

profile of v0, /device:TPU:1, one launch (start us, length us, event | category | flops | bytes accessed | tf_op | source)
XLA Modules:
  0.0 806.1 jit_solution(5505076549163768572)
XLA Ops:
  7.9 11.5 %all-to-all-start = ((bf16[4,128,1536]{2,0,1:T(4,128)(2,1)}), bf16[4,128,1536]{2,0,1:T(4,128)(2,1)S(1)}, u32[]{:S(2)}, u32[]{:S(2)}) async-start(bf16[4,128,1536]{2,0,1:T(4,128)(2,1)} %bitcast.122), calls=%async_computation | async-start | bytes 3145728 | tf_op jit(solution)/shard_map/all_to_all | solution.py:72
  20.3 75.4 %all-reduce = s32[512]{0:T(512)S(1)} all-reduce(s32[512]{0:T(512)S(1)} %dynamic-update-slice), channel_id=1, replica_groups=mesh['gx'=16,'gy'=8] {'gx','gy'}, use_global_device_ids=true, to_apply=%add | all-reduce | flops 512 | bytes 4096
  97.5 2.8 gather_fusion
  100.3 11.1 %multiply_reduce_fusion = (f32[]{:T(128)}, f32[1024,1536]{1,0:T(8,128)}, f32[1024,1536]{1,0:T(8,128)}) fusion(f32[1024,1536]{1,0:T(8,128)} %param.11, bf16[512,1024]{1,0:T(8,128)(2,1)} %gather_fusion, bf16[512,1536]{1,0:T(8,128)(2,1)S(1)} %all_to_all.17), kind=kOutput, calls=%fused_computation.3 | convolution fusion | flops 1620049920 | bytes 21495812 | tf_op jit(solution)/shard_map/dot_general | solution.py:74
  111.4 64.3 %psum.21 = f32[]{:T(128)} all-reduce(f32[]{:T(128)} %get-tuple-element.2), channel_id=1, replica_groups=mesh['gx'=16,'gy'=8] {'gx','gy'}, use_global_device_ids=true, to_apply=%region_2.0 | all-reduce | flops 1 | bytes 8 | tf_op jit(solution)/shard_map/psum | solution.py:79
  176.3 27.5 %fusion.6 = f32[1024,1024]{1,0:T(8,128)} fusion(f32[]{:T(128)S(6)} %add.53, f32[1024,1536]{1,0:T(8,128)} %get-tuple-element.4, f32[1024,1536]{1,0:T(8,128)} %get-tuple-element.3), kind=kOutput, calls=%fused_computation.13 | convolution fusion | flops 19332071424 | bytes 16777220 | tf_op jit(solution)/shard_map/dot_general | solution.py:20
  204.3 150.7 %all-reduce.4.cloned.1.call-done = f32[1024,1024]{1,0:T(8,128)} async-done(((f32[1024,1024]{1,0:T(8,128)}), f32[1024,1024]{1,0:T(8,128)}) %all-reduce.4.cloned.1.call-update) | async-done | bytes 4194320 | tf_op jit(solution)/shard_map/psum | solution.py:64
  362.6 2.6 constant_dynamic-update-slice_fusion.46
  367.7 2.5 constant_dynamic-update-slice_fusion.30
  380.0 2.6 constant_dynamic-update-slice_fusion.38
  385.0 2.5 constant_dynamic-update-slice_fusion.18
  394.2 2.6 constant_dynamic-update-slice_fusion.37
  406.3 2.5 convolution_dynamic-update-slice_fusion.12
  447.4 2.7 convolution_dynamic-update-slice_fusion.9
  459.7 29.6 %multiply_add_fusion = f32[1024,1536]{1,0:T(8,128)S(1)} fusion(f32[1024,1024]{1,0:T(8,128)} %convolution_dynamic-update-slice_fusion.8, f32[1024,1024]{1,0:T(8,128)} %all-reduce.4.cloned.1.call-done, f32[]{:T(128)S(6)} %add.53, f32[1024,1536]{1,0:T(8,128)} %get-tuple-element.4, f32[1024,1536]{1,0:T(8,128)} %get-tuple-element.3), kind=kOutput, calls=%fused_computation.2 | convolution fusion | flops 19343081472 | bytes 27262980 | tf_op jit(solution)/shard_map/dot_general | solution.py:85
  489.3 2.7 copy-done.6
  491.9 21.7 %fusion.215 = f32[1024,1024]{1,0:T(8,128)} fusion(f32[1024,1536]{1,0:T(8,128)S(1)} %multiply_add_fusion), kind=kOutput, calls=%fused_computation.356 | convolution fusion | flops 19327352832 | bytes 10485760 | tf_op jit(solution)/shard_map/dot_general | solution.py:20
  514.7 152.0 %all-reduce.6.cloned.1.call-done = f32[1024,1024]{1,0:T(8,128)} async-done(((f32[1024,1024]{1,0:T(8,128)}), f32[1024,1024]{1,0:T(8,128)}) %all-reduce.6.cloned.1.call-update) | async-done | bytes 4194320 | tf_op jit(solution)/shard_map/psum | solution.py:64
  674.3 2.6 constant_dynamic-update-slice_fusion.49
  691.6 2.6 constant_dynamic-update-slice_fusion.42
  733.3 2.5 convolution_dynamic-update-slice_fusion.3
  752.5 2.5 constant_dynamic-update-slice_fusion.8
  759.0 2.8 convolution_dynamic-update-slice_fusion.1
  771.3 27.8 %add_multiply_fusion = f32[1024,1536]{1,0:T(8,128)} fusion(f32[1024,1536]{1,0:T(8,128)} %copy-done.6, f32[1024,1024]{1,0:T(8,128)} %convolution_dynamic-update-slice_fusion, f32[1024,1024]{1,0:T(8,128)} %all-reduce.6.cloned.1.call-done, f32[1536]{0:T(1024)S(1)} %broadcast_multiply_fusion), kind=kOutput, calls=%fused_computation.1 | convolution fusion | flops 19335217152 | bytes 20977664 | tf_op jit(solution)/shard_map/dot_general | solution.py:85
  (203 shorter events, 182.4 us)
Async XLA Ops:
  7.2 89.0 %all-gather.3.cloned.1.call-start = ((), (), s32[]{:S(2)}) async-start(), calls=%async_computation.3 | async-start | bytes 1056768 | tf_op jit(solution)/shard_map/all_gather | solution.py:69
  7.9 87.8 %all-to-all-start = ((bf16[4,128,1536]{2,0,1:T(4,128)(2,1)}), bf16[4,128,1536]{2,0,1:T(4,128)(2,1)S(1)}, u32[]{:S(2)}, u32[]{:S(2)}) async-start(bf16[4,128,1536]{2,0,1:T(4,128)(2,1)} %bitcast.122), calls=%async_computation | async-start | bytes 3145728 | tf_op jit(solution)/shard_map/all_to_all | solution.py:72
  19.4 335.6 %all-reduce.4.cloned.1.call-start = ((), (), s32[]{:S(2)}) async-start(), calls=%async_computation.1 | async-start | bytes 8388608 | tf_op jit(solution)/shard_map/psum | solution.py:64
  203.9 462.8 %all-reduce.6.cloned.1.call-start = ((), (), s32[]{:S(2)}) async-start(), calls=%async_computation.2 | async-start | bytes 8388608 | tf_op jit(solution)/shard_map/psum | solution.py:64
  362.6 10.1 %copy-start.2 = (f32[1024,1024]{1,0:T(8,128)S(1)}, f32[1024,1024]{1,0:T(8,128)}, u32[]{:S(2)}) copy-start(f32[1024,1024]{1,0:T(8,128)} %all-reduce.4.cloned.1.call-done) | copy-start | bytes 12582916
  379.9 11.4 %copy-start.3 = (f32[1024,1024]{1,0:T(8,128)S(1)}, f32[1024,1024]{1,0:T(8,128)}, u32[]{:S(2)}) copy-start(f32[1024,1024]{1,0:T(8,128)} %all-reduce.4.cloned.1.call-done) | copy-start | bytes 12582916
  489.3 2.7 copy-start.6
  513.7 0.7 copy-start.4
  513.7 0.7 copy-start.5
  674.3 10.1 %copy-start = (f32[1024,1024]{1,0:T(8,128)S(1)}, f32[1024,1024]{1,0:T(8,128)}, u32[]{:S(2)}) copy-start(f32[1024,1024]{1,0:T(8,128)} %all-reduce.6.cloned.1.call-done) | copy-start | bytes 12582916
  691.6 11.3 %copy-start.1 = (f32[1024,1024]{1,0:T(8,128)S(1)}, f32[1024,1024]{1,0:T(8,128)}, u32[]{:S(2)}) copy-start(f32[1024,1024]{1,0:T(8,128)} %all-reduce.6.cloned.1.call-done) | copy-start | bytes 12582916
Sparse Core Ops, SparseCore 0:
  10.7 75.6 all-gather.2
  204.0 150.9 all-reduce.3
  513.9 152.7 all-reduce.5
where the time goes:
time: 813 us; the launch traced here: 806 us
  waiting for transfers between devices  303 us (37%)
  matrix products  285 us (35%)
  blocking collectives  140 us (17%)
  local copies, waits for them, and re-layouts  49.9 us (6%)
  between operations  15.5 us (2%)
  starting transfers between devices  12 us (1%)
    psum x2, waiting for transfers between devices, summed_gram(): return lax.psum(partial_gram, ('gx', 'gy'))  303 us
    dot_general x72, matrix products, gram_square(): pieces.append(jnp.dot(left, right, precision=lax.Precision.HIGHEST))  168 us
    unnamed x1, blocking collectives  75.4 us
    psum x1, blocking collectives, per_device(): squares = lax.psum(jnp.sum(blended * blended), ('gx', 'gy'))  64.3 us
    dot_general x2, matrix products, per_device(): jnp.dot(poly_matrix, orthogonal, precision=lax.Precision.HIGHEST)  57.3 us
    dot_general x2, matrix products, local_gram(): lax.dot_general(matrix, matrix, (((1,), (1,)), ((), ())), precision=lax.P...  49.3 us
    unnamed x73, local copies, waits for them, and re-layouts  41.4 us
  transfers between devices with their start and end apart: 4, of which 2 were waited for; matrix products, arithmetic and copies ran while one was open for 0% of the time, Pallas kernels for 0%

commit v1 on v0

v1 whole, which is shorter than its diff:
```python
import functools
import math

import jax
import jax.numpy as jnp
from jax import lax
from jax.experimental import pallas as pl
from jax.experimental.pallas import tpu as pltpu
from jax.sharding import PartitionSpec as P

OUT = 196608
MOMENTUM_DECAY = 0.95
EPSILON = 1e-07
NEWTON_A = 3.4445
NEWTON_B = -4.775
NEWTON_C = 2.0315

BLOCK = 256
NBLK = 4
NPAIR = 10
CHUNK = 512
F32 = jnp.float32
BF16 = jnp.bfloat16


def split(value):
    high = value.astype(BF16)
    return high, (value - high.astype(F32)).astype(BF16)


def mxu(left, right):
    return lax.dot_general(left, right, (((1,), (0,)), ((), ())), preferred_element_type=F32)


def mxu_t(left, right):
    return lax.dot_general(left, right, (((1,), (1,)), ((), ())), preferred_element_type=F32)


def pair_of(slot):
    row = lax.rem(slot, NBLK)
    col = lax.rem(row + lax.div(slot, NBLK), NBLK)
    return row, col


def front_kernel(lat_ref, cols_ref, mom_ref, newmom_ref, high_ref, low_ref, gram_ref, tlt_ref):
    step = pl.program_id(0)
    tasks = lat_ref.shape[0]
    width = tlt_ref.shape[0]

    @pl.when(step == 0)
    def _():
        tail = lat_ref[:, width:].astype(F32)
        ids = jnp.sum(tail, axis=1, keepdims=True)
        which = lax.broadcasted_iota(jnp.int32, (tasks, tasks), 1).astype(F32)
        onehot = jnp.where(which == ids, 1.0, 0.0).astype(BF16)
        task_latent = mxu(onehot, lat_ref[:, :width])
        tlt_ref[...] = task_latent.T.astype(BF16)
        gram_ref[...] = jnp.zeros_like(gram_ref)

    for i in range(NBLK):
        rows = slice(i * BLOCK, (i + 1) * BLOCK)
        head = mxu(tlt_ref[rows, :], cols_ref[...])
        new_momentum = MOMENTUM_DECAY * mom_ref[rows, :] + head
        newmom_ref[rows, :] = new_momentum
        high, low = split(head + MOMENTUM_DECAY * new_momentum)
        high_ref[rows, :] = high
        low_ref[rows, :] = low

    def body(slot, carry):
        row, col = pair_of(slot)
        rows = pl.ds(pl.multiple_of(row * BLOCK, BLOCK), BLOCK)
        cols = pl.ds(pl.multiple_of(col * BLOCK, BLOCK), BLOCK)
        gram_ref[slot] += (
            mxu_t(high_ref[rows, :], high_ref[cols, :])
            + mxu_t(high_ref[rows, :], low_ref[cols, :])
            + mxu_t(low_ref[rows, :], high_ref[cols, :])
        )
        return carry

    lax.fori_loop(0, NPAIR, body, 0)


def front(lat, cols, momentum):
    width, count = momentum.shape
    tasks = lat.shape[0]
    grid = count // CHUNK
    return pl.pallas_call(
        front_kernel,
        grid=(grid,),
        in_specs=[
            pl.BlockSpec(lat.shape, lambda c: (0, 0)),
            pl.BlockSpec((tasks, CHUNK), lambda c: (0, c)),
            pl.BlockSpec((width, CHUNK), lambda c: (0, c)),
        ],
        out_specs=[
            pl.BlockSpec((width, CHUNK), lambda c: (0, c)),
            pl.BlockSpec((width, CHUNK), lambda c: (0, c)),
            pl.BlockSpec((width, CHUNK), lambda c: (0, c)),
            pl.BlockSpec((NPAIR, BLOCK, BLOCK), lambda c: (0, 0, 0)),
        ],
        out_shape=[
            jax.ShapeDtypeStruct((width, count), F32),
            jax.ShapeDtypeStruct((width, count), BF16),
            jax.ShapeDtypeStruct((width, count), BF16),
            jax.ShapeDtypeStruct((NPAIR, BLOCK, BLOCK), F32),
        ],
        scratch_shapes=[pltpu.VMEM((width, tasks), BF16)],
        compiler_params=pltpu.CompilerParams(vmem_limit_bytes=60 << 20),
        name="front",
    )(lat, cols, momentum)


def back_kernel(gram_ref, high_ref, low_ref, scale_ref, step_ref, inv_ref, mats_ref):
    G, M1, T, G2 = 0, 1, 2, 3

    def store(which, row, col, value):
        high, low = split(value)
        rows = pl.ds(pl.multiple_of(row * BLOCK, BLOCK), BLOCK)
        cols = pl.ds(pl.multiple_of(col * BLOCK, BLOCK), BLOCK)
        mats_ref[which, 0, col, rows, :] = high
        mats_ref[which, 1, col, rows, :] = low
        flipped, flipped_low = split(value.T)
        mats_ref[which, 0, row, cols, :] = flipped
        mats_ref[which, 1, row, cols, :] = flipped_low

    def eye(row, col):
        r = lax.broadcasted_iota(jnp.int32, (BLOCK, BLOCK), 0)
        c = lax.broadcasted_iota(jnp.int32, (BLOCK, BLOCK), 1)
        return jnp.where((r == c) & (row == col), 1.0, 0.0)

    def product(left, right, row, col):
        rows = pl.ds(pl.multiple_of(row * BLOCK, BLOCK), BLOCK)
        total = None
        for k in range(NBLK):
            ks = slice(k * BLOCK, (k + 1) * BLOCK)
            lh, ll = mats_ref[left, 0, k, rows, :], mats_ref[left, 1, k, rows, :]
            rh, rl = mats_ref[right, 0, col, ks, :], mats_ref[right, 1, col, ks, :]
            term = mxu(lh, rh) + mxu(lh, rl) + mxu(ll, rh)
            total = term if total is None else total + term
        return total

    def stage(left, right, dest, finish):
        def body(slot, carry):
            row, col = pair_of(slot)
            store(dest, row, col, finish(slot, row, col, product(left, right, row, col)))
            return carry

        lax.fori_loop(0, NPAIR, body, 0)

    @pl.when(pl.program_id(0) == 0)
    def _():
        r = lax.broadcasted_iota(jnp.int32, (BLOCK, BLOCK), 0)
        c = lax.broadcasted_iota(jnp.int32, (BLOCK, BLOCK), 1)
        diagonal = gram_ref[0] + gram_ref[1] + gram_ref[2] + gram_ref[3]
        picked = jnp.where(r == c, diagonal, 0.0)
        squares = jnp.sum(jnp.sum(picked, axis=1, keepdims=True), axis=0, keepdims=True)
        inverse = 1.0 / (jnp.sqrt(squares) + EPSILON)
        inv_ref[...] = jnp.broadcast_to(inverse, inv_ref.shape)

        def normalise(slot, carry):
            row, col = pair_of(slot)
            inv = inv_ref[0:1, 0:1]
            store(G, row, col, (gram_ref[slot] * inv) * inv)
            return carry

        lax.fori_loop(0, NPAIR, normalise, 0)

        def first(slot, row, col, value):
            inv = inv_ref[0:1, 0:1]
            return NEWTON_A * eye(row, col) + NEWTON_B * ((gram_ref[slot] * inv) * inv) + NEWTON_C * value

        def second(slot, row, col, value):
            rows = pl.ds(pl.multiple_of(row * BLOCK, BLOCK), BLOCK)
            own = mats_ref[G2, 0, col, rows, :].astype(F32) + mats_ref[G2, 1, col, rows, :].astype(F32)
            return NEWTON_A * eye(row, col) + NEWTON_B * own + NEWTON_C * value

        plain = lambda slot, row, col, value: value
        stage(G, G, M1, first)
        stage(G, M1, T, plain)
        stage(T, M1, G2, plain)
        stage(G2, G2, G, second)
        stage(G, M1, T, plain)

    factor = scale_ref[...] * (math.sqrt(OUT) * inv_ref[0:1, 0:1])
    for i in range(NBLK):
        rows = slice(i * BLOCK, (i + 1) * BLOCK)
        total = None
        for k in range(NBLK):
            ks = slice(k * BLOCK, (k + 1) * BLOCK)
            mh, ml = mats_ref[T, 0, k, rows, :], mats_ref[T, 1, k, rows, :]
            term = mxu(mh, high_ref[ks, :]) + mxu(mh, low_ref[ks, :]) + mxu(ml, high_ref[ks, :])
            total = term if total is None else total + term
        step_ref[rows, :] = total * factor


def back(gram, high, low, scale):
    width, count = high.shape
    return pl.pallas_call(
        back_kernel,
        grid=(count // CHUNK,),
        in_specs=[
            pl.BlockSpec(gram.shape, lambda c: (0, 0, 0)),
            pl.BlockSpec((width, CHUNK), lambda c: (0, c)),
            pl.BlockSpec((width, CHUNK), lambda c: (0, c)),
            pl.BlockSpec((1, CHUNK), lambda c: (0, c)),
        ],
        out_specs=pl.BlockSpec((width, CHUNK), lambda c: (0, c)),
        out_shape=jax.ShapeDtypeStruct((width, count), F32),
        scratch_shapes=[
            pltpu.VMEM((8, 128), F32),
            pltpu.VMEM((4, 2, NBLK, width, BLOCK), BF16),
        ],
        compiler_params=pltpu.CompilerParams(vmem_limit_bytes=60 << 20),
        name="back",
    )(gram, high, low, scale)


def per_device(factor_grads, latents, task_ids, offsets, target_scale, momentum):
    axes = ("gx", "gy")
    rows = latents.shape[0]
    low_part = task_ids % 16
    tail = jnp.stack([task_ids - low_part, low_part], axis=1).astype(BF16)
    tail = jnp.pad(tail, ((0, 0), (0, 126)))
    lat = lax.all_gather(jnp.concatenate([latents, tail], axis=1), axes, axis=0, tiled=True)
    columns = lax.all_to_all(factor_grads, axes, split_axis=1, concat_axis=0, tiled=True)
    new_momentum, high, low, gram = front(lat, columns, momentum)
    count = momentum.shape[1]
    column_index = lax.axis_index(axes) * count + jnp.arange(count, dtype=jnp.int32)
    following = jnp.concatenate([offsets[1:], jnp.full((1,), OUT, jnp.int32)])
    inside = (column_index[None, :] >= offsets[:, None]) & (column_index[None, :] < following[:, None])
    column_scale = jnp.sum(jnp.where(inside, target_scale[:, None], 0.0), axis=0)[None, :]
    gram = lax.psum(gram, axes)
    return new_momentum, back(gram, high, low, column_scale)


def solution(mesh):
    placed = (
        P(("gx", "gy"), None),
        P(("gx", "gy"), None),
        P(("gx", "gy")),
        P(),
        P(),
        P(None, ("gx", "gy")),
    )
    return jax.shard_map(
        per_device,
        mesh=mesh,
        in_specs=placed,
        out_specs=(P(None, ("gx", "gy")), P(None, ("gx", "gy"))),
        check_vma=False,
    )
```

time: 813 us -> 317 us (0.39)
  matrix products: 285 us -> 0 us
  waiting for transfers between devices: 303 us -> 189 us
  blocking collectives: 140 us -> 36.2 us
  Pallas kernels: 0 us -> 69.5 us
  local copies, waits for them, and re-layouts: 49.9 us -> 5.85 us
  starting transfers between devices: 12 us -> 0.08 us
    dot_general x77 -> x0, matrix products: 285 us -> none  [the longest x72 168 us: gram_square(): pieces.append(jnp.dot(left, right, precision=lax.Precision.HIGHEST))]
    psum x2 -> x1, waiting for transfers between devices: 303 us -> 148 us  [per_device(): gram = lax.psum(gram, axes)]
    unnamed x1 -> x0, blocking collectives: 75.4 us -> none
    pallas_call x0 -> x2, Pallas kernels: none -> 69.5 us  [the longest x1 48.9 us: back(): pl.pallas_call(back_kernel, grid=(count // CHUNK,), in_specs=[pl.BlockSpe...]
    psum x1 -> x0, blocking collectives: 64.3 us -> none  [per_device(): squares = lax.psum(jnp.sum(blended * blended), ('gx', 'gy'))]
    all_gather x1, waiting for transfers between devices: 0.02 us -> 41.2 us  [per_device(): lax.all_gather(jnp.concatenate([latents, tail], axis=1), axes, axis=0, ti...]
    unnamed x73 -> x6, local copies, waits for them, and re-layouts: 41.4 us -> 3.87 us
    all_to_all x0 -> x1, blocking collectives: none -> 36.2 us  [per_device(): lax.all_to_all(factor_grads, axes, split_axis=1, concat_axis=0, tiled=True)]
  transfers between devices with their start and end apart: 4 -> 2, of which waited for: 2 -> 2; matrix products, arithmetic and copies ran while one was open for 0% -> 0% of each run, Pallas kernels for 0% -> 0%
where the time goes in v1:
time: 317 us
  waiting for transfers between devices  189 us (60%)
  Pallas kernels  69.5 us (22%)
  blocking collectives  36.2 us (11%)
  between operations  14.1 us (4%)
  local copies, waits for them, and re-layouts  5.85 us (2%)
    psum x1, waiting for transfers between devices, per_device(): gram = lax.psum(gram, axes)  148 us
    pallas_call x1, Pallas kernels, back(): pl.pallas_call(back_kernel, grid=(count // CHUNK,), in_specs=[pl.BlockSpe...  48.9 us
    all_gather x1, waiting for transfers between devices, per_device(): lax.all_gather(jnp.concatenate([latents, tail], axis=1), axes, axis=0, ti...  41.2 us
    all_to_all x1, blocking collectives, per_device(): lax.all_to_all(factor_grads, axes, split_axis=1, concat_axis=0, tiled=True)  36.2 us
    pallas_call x1, Pallas kernels, front(): pl.pallas_call(front_kernel, grid=(grid,), in_specs=[pl.BlockSpec(lat.sha...  20.6 us
  transfers between devices with their start and end apart: 2, of which 2 were waited for; matrix products, arithmetic and copies ran while one was open for 0% of the time, Pallas kernels for 0%

profile of v1, /device:TPU:1, one launch (start us, length us, event | category | flops | bytes accessed | tf_op | source)
XLA Modules:
  0.0 317.0 jit_solution(234423761457704254)
XLA Ops:
  7.2 0.0 all-gather.3.cloned.1.call-start
  7.2 0.7 convert_bitcast_fusion.1
  7.9 0.1 copy.14
  8.0 1.3 fusion.2
  9.3 0.0 all-gather.3.cloned.1.call-update
  9.3 0.0 all-reduce.3.cloned.1.call-start
  9.4 36.2 %all_to_all.19 = bf16[4,128,1536]{2,0,1:T(4,128)(2,1)S(1)} all-to-all(bf16[4,128,1536]{2,0,1:T(4,128)(2,1)} %bitcast.9), channel_id=1, replica_groups=mesh['gx'=16,'gy'=8] {'gx','gy'}, dimensions={1} | all-to-all | bytes 3145728 | tf_op jit(solution)/shard_map/all_to_all | solution.py:225
  45.6 1.3 all_to_all.17.cols_ref
  46.9 41.2 %all-gather.3.cloned.1.call-done = bf16[128,4,1152]{2,1,0:T(4,128)(2,1)} async-done(((bf16[1,4,1152]{2,1,0:T(4,128)(2,1)}), bf16[128,4,1152]{2,1,0:T(4,128)(2,1)}) %all-gather.3.cloned.1.call-update) | async-done | bytes 1179664 | tf_op jit(solution)/shard_map/all_gather | solution.py:224
  88.0 3.1 reshape.15.lat_ref
  91.2 20.6 %front.1 = (f32[1024,1536]{1,0:T(8,128)}, bf16[1024,1536]{1,0:T(8,128)(2,1)}, bf16[1024,1536]{1,0:T(8,128)(2,1)}, f32[10,256,256]{2,1,0:T(8,128)}) custom-call(bf16[512,1152]{1,0:T(8,128)(2,1)} %reshape.15.lat_ref, bf16[512,1536]{1,0:T(8,128)(2,1)} %all_to_all.17.cols_ref, f32[1024,1536]{1,0:T(8,128)} %mom_ref.1), custom_call_target="tpu_custom_call" | custom-call | tf_op jit(solution)/shard_map/front/pallas_call | solution.py:87
  111.8 0.0 copy-start
  111.8 0.0 copy-start.1
  111.8 0.0 all-reduce.3.cloned.1.call-update
  111.9 0.6 copy-done
  112.5 0.1 slice.3
  112.6 0.1 pad_add_fusion
  112.6 0.0 copy-done.1
  112.6 0.2 select_reduce_fusion
  112.9 0.6 broadcast_in_dim.22.scale_ref
  113.5 147.8 %all-reduce.3.cloned.1.call-done.gram_ref = f32[10,256,256]{2,1,0:T(8,128)} async-done(((f32[10,256,256]{2,1,0:T(8,128)}), f32[10,256,256]{2,1,0:T(8,128)}) %all-reduce.3.cloned.1.call-update) | async-done | bytes 2621456 | tf_op jit(solution)/shard_map/psum | solution.py:232
  261.3 48.9 %back.1 = f32[1024,1536]{1,0:T(8,128)} custom-call(f32[10,256,256]{2,1,0:T(8,128)} %all-reduce.3.cloned.1.call-done.gram_ref, bf16[1024,1536]{1,0:T(8,128)(2,1)} %get-tuple-element.8.high_ref, bf16[1024,1536]{1,0:T(8,128)(2,1)} %get-tuple-element.9.low_ref, f32[1,1536]{1,0:T(1,128)} %broadcast_in_dim.22.scale_ref), custom_call_target="tpu_custom_call" | custom-call | tf_op jit(solution)/shard_map/back/pallas_call | solution.py:198
  (3 shorter events, 0.0 us)
Async XLA Ops:
  7.2 80.9 %all-gather.3.cloned.1.call-start = ((), (), s32[]{:S(2)}) async-start(), calls=%async_computation.2 | async-start | bytes 1188864 | tf_op jit(solution)/shard_map/all_gather | solution.py:224
  9.3 252.0 %all-reduce.3.cloned.1.call-start = ((), (), s32[]{:S(2)}) async-start(), calls=%async_computation.1 | async-start | bytes 5242880 | tf_op jit(solution)/shard_map/psum | solution.py:232
  111.8 0.7 copy-start
  111.8 0.8 copy-start.1
Sparse Core Ops, SparseCore 0:
  11.3 76.6 all-gather.2
  112.0 149.2 all-reduce.2

commit v2 on v1

--- a/solution.py
+++ b/solution.py
@@ -1,4 +1,3 @@
-import functools
 import math
 
 import jax
@@ -19,8 +18,271 @@
 NBLK = 4
 NPAIR = 10
 CHUNK = 512
+PACKED = 36 * 128
 F32 = jnp.float32
 BF16 = jnp.bfloat16
+MESH = pl.DeviceIdType.MESH
+
+
+def place():
+    gx = lax.axis_index("gx")
+    gy = lax.axis_index("gy")
+    return lax.div(gx, 4), lax.rem(gx, 4), lax.div(gy, 2), lax.rem(gy, 2)
+
+
+def peer_of(where, axis, hop):
+    x, z, y, core = where
+    if axis == 0:
+        x = lax.rem(x + hop, 4)
+    elif axis == 1:
+        y = lax.rem(y + hop, 4)
+    elif axis == 2:
+        z = lax.rem(z + hop, 4)
+    else:
+        core = 1 - core
+    return (x * 4 + z, y * 2 + core)
+
+
+PIECE = 48
+
+
+def reduce_kernel(in_ref, out_ref, half_ref, from_core, got1, sum1, got2, sum2, got3,
+                  cs, cr, s1, r1, s2, r2, s3, r3, s4, r4, s5, r5, s6, r6):
+    where = place()
+    x, z, y, core = where
+    coord = (x, y, z)
+    barrier = pltpu.get_barrier_semaphore()
+    partners = [peer_of(where, 3, 1)] + [peer_of(where, a, k) for a in range(3) for k in (1, 2, 3)]
+    for p in partners:
+        pl.semaphore_signal(barrier, inc=1, device_id=p, device_id_type=MESH)
+    pl.semaphore_wait(barrier, len(partners))
+
+    def remote(src, dst, ssem, rsem, dev):
+        return pltpu.make_async_remote_copy(src_ref=src, dst_ref=dst, send_sem=ssem, recv_sem=rsem,
+                                            device_id=dev, device_id_type=MESH)
+
+    other = 1 - core
+    started = []
+    first = []
+    for r in range(3):
+        c = remote(in_ref.at[r, other], from_core.at[r], cs.at[r], cr.at[r], peer_of(where, 3, 1))
+        c.start()
+        first.append(c)
+        started.append(c)
+    hops = (2, 1, 3)
+    phase = []
+    for r in range(3):
+        first[r].wait_recv()
+        half_ref[r] = in_ref[r, core] + from_core[r]
+        mine = []
+        for k in hops:
+            to = lax.rem(coord[r] + k, 4)
+            c = remote(half_ref.at[r, to], got1.at[r, k - 1], s1.at[r, k - 1], r1.at[r, k - 1], peer_of(where, r, k))
+            c.start()
+            mine.append(c)
+        phase.append(mine)
+        started += mine
+    phase2 = []
+    for r in range(3):
+        b = (r + 1) % 3
+        for c in phase[r]:
+            c.wait_recv()
+        sum1[r] = (half_ref[r, coord[r]] + got1[r, 0]) + (got1[r, 1] + got1[r, 2])
+        mine = []
+        for k in hops:
+            to = lax.rem(coord[b] + k, 4)
+            c = remote(sum1.at[r, to], got2.at[r, k - 1], s2.at[r, k - 1], r2.at[r, k - 1], peer_of(where, b, k))
+            c.start()
+            mine.append(c)
+        phase2.append(mine)
+        started += mine
+    phase3 = []
+    for r in range(3):
+        b, d = (r + 1) % 3, (r + 2) % 3
+        for c in phase2[r]:
+            c.wait_recv()
+        sum2[r] = (sum1[r, coord[b]] + got2[r, 0]) + (got2[r, 1] + got2[r, 2])
+        mine = []
+        for k in hops:
+            c = remote(sum2.at[r], got3.at[r, k - 1], s3.at[r, k - 1], r3.at[r, k - 1], peer_of(where, d, k))
+            c.start()
+            mine.append(c)
+        phase3.append(mine)
+        started += mine
+    phase4 = []
+    for r in range(3):
+        b = (r + 1) % 3
+        for c in phase3[r]:
+            c.wait_recv()
+        out_ref[r, core, coord[r], coord[b]] = (sum2[r] + got3[r, 0]) + (got3[r, 1] + got3[r, 2])
+        own = out_ref.at[r, core, coord[r], coord[b]]
+        mine = []
+        for k in hops:
+            c = remote(own, own, s4.at[r, k - 1], r4.at[r, k - 1], peer_of(where, b, k))
+            c.start()
+            mine.append(c)
+        phase4.append(mine)
+        started += mine
+    phase5 = []
+    for r in range(3):
+        for c in phase4[r]:
+            c.wait_recv()
+        own = out_ref.at[r, core, coord[r]]
+        mine = []
+        for k in hops:
+            c = remote(own, own, s5.at[r, k - 1], r5.at[r, k - 1], peer_of(where, r, k))
+            c.start()
+            mine.append(c)
+        phase5.append(mine)
+        started += mine
+    last = []
+    for r in range(3):
+        for c in phase5[r]:
+            c.wait_recv()
+        own = out_ref.at[r, core]
+        c = remote(own, own, s6.at[r], r6.at[r], peer_of(where, 3, 1))
+        c.start()
+        last.append(c)
+        started.append(c)
+    for c in last:
+        c.wait_recv()
+    for c in started:
+        c.wait_send()
+
+
+def reduce_gram(gram):
+    shape = (3, 2, 4, 4, PIECE, 128)
+    dma = pltpu.SemaphoreType.DMA
+    out = pl.pallas_call(
+        reduce_kernel,
+        in_specs=[pl.BlockSpec(memory_space=pltpu.VMEM)],
+        out_specs=pl.BlockSpec(memory_space=pltpu.VMEM),
+        out_shape=jax.ShapeDtypeStruct(shape, F32),
+        scratch_shapes=[
+            pltpu.VMEM((3, 4, 4, PIECE, 128), F32),
+            pltpu.VMEM((3, 4, 4, PIECE, 128), F32),
+            pltpu.VMEM((3, 3, 4, PIECE, 128), F32),
+            pltpu.VMEM((3, 4, PIECE, 128), F32),
+            pltpu.VMEM((3, 3, PIECE, 128), F32),
+            pltpu.VMEM((3, PIECE, 128), F32),
+            pltpu.VMEM((3, 3, PIECE, 128), F32),
+            dma((3,)), dma((3,)),
+        ] + [dma((3, 3))] * 10 + [dma((3,)), dma((3,))],
+        compiler_params=pltpu.CompilerParams(collective_id=1, has_side_effects=True),
+        name="reduce_gram",
+    )(gram.reshape(shape))
+    return out.reshape(gram.shape)
+
+
+def exchange_kernel(grads_ref, lat_ref, ids_ref, offsets_ref, scales_ref,
+                    cols_ref, lats_ref, scale_ref, own_ref,
+                    gs, gr, own_sem, s1, r1, s2, r2, s3, r3, s4, r4):
+    where = place()
+    x, z, y, core = where
+    count = cols_ref.shape[2]
+    total = cols_ref.shape[0]
+    rows, width = lat_ref.shape
+    me = lax.axis_index("gx") * 8 + lax.axis_index("gy")
+    barrier = pltpu.get_barrier_semaphore()
+
+    def device(to):
+        return (lax.div(to, 8), lax.rem(to, 8))
+
+    def greet(k, carry):
+        pl.semaphore_signal(barrier, inc=1, device_id=device(lax.rem(me + k, total)), device_id_type=MESH)
+        return carry
+
+    lax.fori_loop(1, total, greet, 0)
+
+    own_ref[:, :width] = lat_ref[...]
+    at_row = lax.broadcasted_iota(jnp.int32, (rows, 128), 0)
+    at_lane = lax.broadcasted_iota(jnp.int32, (rows, 128), 1)
+    ids = jnp.zeros((rows, 128), jnp.int32)
+    for r in range(rows):
+        ids = jnp.where(at_row == r, ids_ref[r], ids)
+    fine = jnp.bitwise_and(ids, 15)
+    tail = jnp.where(at_lane == 0, ids - fine, jnp.where(at_lane == 1, fine, 0))
+    own_ref[:, width:] = tail.astype(F32).astype(BF16)
+
+    column = me * count + 128 * lax.broadcasted_iota(jnp.int32, scale_ref.shape, 0)
+    column = column + lax.broadcasted_iota(jnp.int32, scale_ref.shape, 1)
+
+    def level(t, value):
+        return jnp.where(column >= offsets_ref[t], scales_ref[t], value)
+
+    scale_ref[...] = lax.fori_loop(0, offsets_ref.shape[0], level, jnp.zeros(scale_ref.shape, F32))
+
+    pl.semaphore_wait(barrier, total - 1)
+
+    def remote(src, dst, ssem, rsem, dev):
+        copy = pltpu.make_async_remote_copy(
+            src_ref=src, dst_ref=dst, send_sem=ssem, recv_sem=rsem, device_id=dev, device_id_type=MESH)
+        copy.start()
+        return copy
+
+    keep = pltpu.make_async_copy(own_ref, lats_ref.at[x, z, y, core], own_sem)
+    keep.start()
+    started = []
+    first = [remote(own_ref, lats_ref.at[x, z, y, core], s1.at[k - 1], r1.at[k - 1], peer_of(where, 1, k))
+             for k in (2, 1, 3)]
+    own = pltpu.make_async_copy(
+        grads_ref.at[:, pl.ds(pl.multiple_of(me * count, count), count)], cols_ref.at[me], gr)
+    own.start()
+
+    def send(k, carry):
+        to = lax.rem(me + lax.rem(k * 37, total), total)
+        pltpu.make_async_remote_copy(
+            src_ref=grads_ref.at[:, pl.ds(pl.multiple_of(to * count, count), count)],
+            dst_ref=cols_ref.at[me], send_sem=gs, recv_sem=gr,
+            device_id=device(to), device_id_type=MESH).start()
+        return carry
+
+    lax.fori_loop(1, 24, send, 0)
+    keep.wait()
+    for copy in first:
+        copy.wait_recv()
+    part = lats_ref.at[x, z, :, core]
+    second = [remote(part, part, s2.at[k - 1], r2.at[k - 1], peer_of(where, 2, k)) for k in (2, 1, 3)]
+    lax.fori_loop(24, 56, send, 0)
+    for copy in second:
+        copy.wait_recv()
+    part = lats_ref.at[x, :, :, core]
+    third = [remote(part, part, s3.at[k - 1], r3.at[k - 1], peer_of(where, 0, k)) for k in (2, 1, 3)]
+    lax.fori_loop(56, total, send, 0)
+    for copy in third:
+        copy.wait_recv()
+    part = lats_ref.at[:, :, :, core]
+    last = remote(part, part, s4, r4, peer_of(where, 3, 1))
+    last.wait_recv()
+    pltpu.make_async_copy(cols_ref, cols_ref, gr).wait()
+    rest = cols_ref.at[pl.ds(0, total - 1)]
+    pltpu.make_async_copy(rest, rest, gs).wait()
+    for copy in first + second + third + [last]:
+        copy.wait_send()
+
+
+def exchange(grads, lat, ids, offsets, scales):
+    total = 128
+    rows, width = lat.shape
+    count = grads.shape[1] // total
+    dma = pltpu.SemaphoreType.DMA
+    smem = pl.BlockSpec(memory_space=pltpu.SMEM)
+    vmem = pl.BlockSpec(memory_space=pltpu.VMEM)
+    anywhere = pl.BlockSpec(memory_space=pl.ANY)
+    return pl.pallas_call(
+        exchange_kernel,
+        in_specs=[anywhere, vmem, smem, smem, smem],
+        out_specs=[anywhere, vmem, vmem],
+        out_shape=[
+            jax.ShapeDtypeStruct((total, rows, count), grads.dtype),
+            jax.ShapeDtypeStruct((4, 4, 4, 2, rows, width + 128), lat.dtype),
+            jax.ShapeDtypeStruct((count // 128, 128), F32),
+        ],
+        scratch_shapes=[pltpu.VMEM((rows, width + 128), lat.dtype), dma, dma, dma]
+        + [dma((3,))] * 6 + [dma, dma],
+        compiler_params=pltpu.CompilerParams(collective_id=2, has_side_effects=True),
+        name="exchange",
+    )(grads, lat, ids, offsets, scales)
 
 
 def split(value):
@@ -42,7 +304,15 @@
     return row, col
 
 
-def front_kernel(lat_ref, cols_ref, mom_ref, newmom_ref, high_ref, low_ref, gram_ref, tlt_ref):
+def quarters(slot):
+    return ((0, 0), (0, 1), (1, 1)) if slot < NBLK else ((0, 0), (0, 1), (1, 0), (1, 1))
+
+
+def first_of(slot):
+    return 3 * slot if slot < NBLK else 3 * NBLK + 4 * (slot - NBLK)
+
+
+def front_kernel(lat_ref, cols_ref, mom_ref, newmom_ref, high_ref, low_ref, packed_ref, tlt_ref, gram_ref):
     step = pl.program_id(0)
     tasks = lat_ref.shape[0]
     width = tlt_ref.shape[0]
@@ -78,6 +348,14 @@
         return carry
 
     lax.fori_loop(0, NPAIR, body, 0)
+
+    @pl.when(step == pl.num_programs(0) - 1)
+    def _():
+        half = BLOCK // 2
+        for slot in range(NPAIR):
+            for at, (r, c) in enumerate(quarters(slot)):
+                base = (first_of(slot) + at) * half
+                packed_ref[base : base + half, :] = gram_ref[slot, r * half : (r + 1) * half, c * half : (c + 1) * half]
 
 
 def front(lat, cols, momentum):
@@ -96,15 +374,15 @@
             pl.BlockSpec((width, CHUNK), lambda c: (0, c)),
             pl.BlockSpec((width, CHUNK), lambda c: (0, c)),
             pl.BlockSpec((width, CHUNK), lambda c: (0, c)),
-            pl.BlockSpec((NPAIR, BLOCK, BLOCK), lambda c: (0, 0, 0)),
+            pl.BlockSpec((PACKED, 128), lambda c: (0, 0)),
         ],
         out_shape=[
             jax.ShapeDtypeStruct((width, count), F32),
             jax.ShapeDtypeStruct((width, count), BF16),
             jax.ShapeDtypeStruct((width, count), BF16),
-            jax.ShapeDtypeStruct((NPAIR, BLOCK, BLOCK), F32),
+            jax.ShapeDtypeStruct((PACKED, 128), F32),
         ],
-        scratch_shapes=[pltpu.VMEM((width, tasks), BF16)],
+        scratch_shapes=[pltpu.VMEM((width, tasks), BF16), pltpu.VMEM((NPAIR, BLOCK, BLOCK), F32)],
         compiler_params=pltpu.CompilerParams(vmem_limit_bytes=60 << 20),
         name="front",
     )(lat, cols, momentum)
@@ -112,6 +390,15 @@
 
 def back_kernel(gram_ref, high_ref, low_ref, scale_ref, step_ref, inv_ref, mats_ref):
     G, M1, T, G2 = 0, 1, 2, 3
+
+    def unpack(slot):
+        half = BLOCK // 2
+        base = first_of(slot) * half
+        part = [gram_ref[base + at * half : base + (at + 1) * half, :] for at in range(len(quarters(slot)))]
+        if slot < NBLK:
+            part = [part[0], part[1], part[1].T, part[2]]
+        top = jnp.concatenate(part[:2], axis=1)
+        return jnp.concatenate([top, jnp.concatenate(part[2:], axis=1)], axis=0)
 
     def store(which, row, col, value):
         high, low = split(value)
@@ -151,37 +438,36 @@
     def _():
         r = lax.broadcasted_iota(jnp.int32, (BLOCK, BLOCK), 0)
         c = lax.broadcasted_iota(jnp.int32, (BLOCK, BLOCK), 1)
-        diagonal = gram_ref[0] + gram_ref[1] + gram_ref[2] + gram_ref[3]
+        diagonal = unpack(0) + unpack(1) + unpack(2) + unpack(3)
         picked = jnp.where(r == c, diagonal, 0.0)
         squares = jnp.sum(jnp.sum(picked, axis=1, keepdims=True), axis=0, keepdims=True)
         inverse = 1.0 / (jnp.sqrt(squares) + EPSILON)
         inv_ref[...] = jnp.broadcast_to(inverse, inv_ref.shape)
 
-        def normalise(slot, carry):
-            row, col = pair_of(slot)
-            inv = inv_ref[0:1, 0:1]
-            store(G, row, col, (gram_ref[slot] * inv) * inv)
-            return carry
-
-        lax.fori_loop(0, NPAIR, normalise, 0)
-
-        def first(slot, row, col, value):
-            inv = inv_ref[0:1, 0:1]
-            return NEWTON_A * eye(row, col) + NEWTON_B * ((gram_ref[slot] * inv) * inv) + NEWTON_C * value
-
-        def second(slot, row, col, value):
-            rows = pl.ds(pl.multiple_of(row * BLOCK, BLOCK), BLOCK)
-            own = mats_ref[G2, 0, col, rows, :].astype(F32) + mats_ref[G2, 1, col, rows, :].astype(F32)
-            return NEWTON_A * eye(row, col) + NEWTON_B * own + NEWTON_C * value
+        for slot in range(NPAIR):
+            row = slot % NBLK
+            store(G, row, (row + slot // NBLK) % NBLK, (unpack(slot) * inverse) * inverse)
+
+        def newton(which):
+            def finish(slot, row, col, value):
+                rows = pl.ds(pl.multiple_of(row * BLOCK, BLOCK), BLOCK)
+                own = mats_ref[which, 0, col, rows, :].astype(F32) + mats_ref[which, 1, col, rows, :].astype(F32)
+                return NEWTON_A * eye(row, col) + NEWTON_B * own + NEWTON_C * value
+
+            return finish
 
         plain = lambda slot, row, col, value: value
-        stage(G, G, M1, first)
+        stage(G, G, M1, newton(G))
         stage(G, M1, T, plain)
         stage(T, M1, G2, plain)
-        stage(G2, G2, G, second)
+        stage(G2, G2, G, newton(G2))
         stage(G, M1, T, plain)
 
-    factor = scale_ref[...] * (math.sqrt(OUT) * inv_ref[0:1, 0:1])
+    width = CHUNK // 128
+    factor = [
+        scale_ref[pl.ds(pl.program_id(0) * width + at, 1), :] * (math.sqrt(OUT) * inv_ref[0:1, 0:1])
+        for at in range(width)
+    ]
     for i in range(NBLK):
         rows = slice(i * BLOCK, (i + 1) * BLOCK)
         total = None
@@ -190,7 +476,9 @@
             mh, ml = mats_ref[T, 0, k, rows, :], mats_ref[T, 1, k, rows, :]
             term = mxu(mh, high_ref[ks, :]) + mxu(mh, low_ref[ks, :]) + mxu(ml, high_ref[ks, :])
             total = term if total is None else total + term
-        step_ref[rows, :] = total * factor
+        for at in range(width):
+            lanes = slice(at * 128, (at + 1) * 128)
+            step_ref[rows, lanes] = total[:, lanes] * factor[at]
 
 
 def back(gram, high, low, scale):
@@ -199,10 +487,10 @@
         back_kernel,
         grid=(count // CHUNK,),
         in_specs=[
-            pl.BlockSpec(gram.shape, lambda c: (0, 0, 0)),
+            pl.BlockSpec(gram.shape, lambda c: (0, 0)),
             pl.BlockSpec((width, CHUNK), lambda c: (0, c)),
             pl.BlockSpec((width, CHUNK), lambda c: (0, c)),
-            pl.BlockSpec((1, CHUNK), lambda c: (0, c)),
+            pl.BlockSpec(scale.shape, lambda c: (0, 0)),
         ],
         out_specs=pl.BlockSpec((width, CHUNK), lambda c: (0, c)),
         out_shape=jax.ShapeDtypeStruct((width, count), F32),
@@ -216,21 +504,11 @@
 
 
 def per_device(factor_grads, latents, task_ids, offsets, target_scale, momentum):
-    axes = ("gx", "gy")
-    rows = latents.shape[0]
-    low_part = task_ids % 16
-    tail = jnp.stack([task_ids - low_part, low_part], axis=1).astype(BF16)
-    tail = jnp.pad(tail, ((0, 0), (0, 126)))
-    lat = lax.all_gather(jnp.concatenate([latents, tail], axis=1), axes, axis=0, tiled=True)
-    columns = lax.all_to_all(factor_grads, axes, split_axis=1, concat_axis=0, tiled=True)
+    columns, lat, column_scale = exchange(factor_grads, latents, task_ids, offsets, target_scale)
+    columns = columns.reshape(-1, columns.shape[-1])
+    lat = lat.reshape(-1, lat.shape[-1])
     new_momentum, high, low, gram = front(lat, columns, momentum)
-    count = momentum.shape[1]
-    column_index = lax.axis_index(axes) * count + jnp.arange(count, dtype=jnp.int32)
-    following = jnp.concatenate([offsets[1:], jnp.full((1,), OUT, jnp.int32)])
-    inside = (column_index[None, :] >= offsets[:, None]) & (column_index[None, :] < following[:, None])
-    column_scale = jnp.sum(jnp.where(inside, target_scale[:, None], 0.0), axis=0)[None, :]
-    gram = lax.psum(gram, axes)
-    return new_momentum, back(gram, high, low, column_scale)
+    return new_momentum, back(reduce_gram(gram), high, low, column_scale)
 
 
 def solution(mesh):

time: 317 us -> 154 us (0.49)
  waiting for transfers between devices: 189 us -> 0 us
  Pallas kernels: 69.5 us -> 148 us
  blocking collectives: 36.2 us -> 0 us
  between operations: 14.1 us -> 0.66 us
    psum x1 -> x0, waiting for transfers between devices: 148 us -> none  [per_device(): gram = lax.psum(gram, axes)]
    pallas_call x0 -> x2, Pallas kernels: none -> 79.8 us  [the longest x1 44.7 us: exchange(): pl.pallas_call(exchange_kernel, in_specs=[anywhere, vmem, smem, smem, sme...]
    all_gather x1 -> x0, waiting for transfers between devices: 41.2 us -> none  [per_device(): lax.all_gather(jnp.concatenate([latents, tail], axis=1), axes, axis=0, ti...]
    all_to_all x1 -> x0, blocking collectives: 36.2 us -> none  [per_device(): lax.all_to_all(factor_grads, axes, split_axis=1, concat_axis=0, tiled=True)]
    reshape x0 -> x2, local copies, waits for them, and re-layouts: none -> 4.57 us  [the longest x1 3.24 us: per_device(): lat = lat.reshape(-1, lat.shape[-1])]
    unnamed x6 -> x2, local copies, waits for them, and re-layouts: 3.87 us -> 0.01 us
  transfers between devices with their start and end apart: 2 -> 0, of which waited for: 2 -> 0; matrix products, arithmetic and copies ran while one was open for 0% -> 0% of each run, Pallas kernels for 0% -> 0%
where the time goes in v2:
time: 154 us; the launch traced here: 153 us
  Pallas kernels  148 us (96%)
  local copies, waits for them, and re-layouts  4.57 us (3%)
    pallas_call x1, Pallas kernels, back(): pl.pallas_call(back_kernel, grid=(count // CHUNK,), in_specs=[pl.BlockSpe...  47.6 us
    pallas_call x1, Pallas kernels, exchange(): pl.pallas_call(exchange_kernel, in_specs=[anywhere, vmem, smem, smem, sme...  44.7 us
    pallas_call x1, Pallas kernels, reduce_gram(): pl.pallas_call(reduce_kernel, in_specs=[pl.BlockSpec(memory_space=pltpu.V...  35.2 us
    pallas_call x1, Pallas kernels, front(): pl.pallas_call(front_kernel, grid=(grid,), in_specs=[pl.BlockSpec(lat.sha...  20.7 us
    reshape x1, local copies, waits for them, and re-layouts, per_device(): lat = lat.reshape(-1, lat.shape[-1])  3.24 us

profile of v2, /device:TPU:1, one launch (start us, length us, event | category | flops | bytes accessed | tf_op | source)
XLA Modules:
  0.0 153.4 jit_solution(8634655710059587350)
XLA Ops:
  0.6 44.7 %exchange.1 = (bf16[128,4,1536]{2,1,0:T(4,128)(2,1)}, bf16[4,4,4,2,4,1152]{5,4,3,2,1,0:T(4,128)(2,1)}, f32[12,128]{1,0:T(8,128)}) custom-call(bf16[4,196608]{1,0:T(4,128)(2,1)} %grads_ref.1, bf16[4,1024]{1,0:T(4,128)(2,1)} %lat_ref.1, s32[4]{0:T(128)} %ids_ref.1, s32[160]{0:T(256)} %offsets_ref.1, f32[160]{0:T(256)} %scales_ref.1), custom_call_target="tpu_custom_call" | custom-call | tf_op jit(solution)/shard_map/exchange/pallas_call | solution.py:272
  45.3 0.0 copy-start
  45.3 3.2 %reshape.16.lat_ref = bf16[512,1152]{1,0:T(8,128)(2,1)} reshape(bf16[4,4,4,2,4,1152]{5,4,3,2,1,0:T(4,128)(2,1)} %get-tuple-element.9) | data formatting | bytes 2359296 | tf_op jit(solution)/shard_map/reshape | solution.py:509
  48.5 0.0 copy-done
  48.5 1.3 reshape.17.cols_ref
  49.9 20.7 %front.1 = (f32[1024,1536]{1,0:T(8,128)}, bf16[1024,1536]{1,0:T(8,128)(2,1)}, bf16[1024,1536]{1,0:T(8,128)(2,1)}, f32[4608,128]{1,0:T(8,128)}) custom-call(bf16[512,1152]{1,0:T(8,128)(2,1)} %reshape.16.lat_ref, bf16[512,1536]{1,0:T(8,128)(2,1)} %reshape.17.cols_ref, f32[1024,1536]{1,0:T(8,128)} %mom_ref.1), custom_call_target="tpu_custom_call" | custom-call | tf_op jit(solution)/shard_map/front/pallas_call | solution.py:365
  70.6 35.2 %reduce_gram.1 = f32[3,2,4,4,48,128]{5,4,3,2,1,0:T(8,128)} custom-call(f32[3,2,4,4,48,128]{5,4,3,2,1,0:T(8,128)} %bitcast.3), custom_call_target="tpu_custom_call" | custom-call | tf_op jit(solution)/shard_map/reduce_gram/pallas_call | solution.py:156
  105.8 47.6 %back.1 = f32[1024,1536]{1,0:T(8,128)} custom-call(f32[4608,128]{1,0:T(8,128)} %bitcast.2, bf16[1024,1536]{1,0:T(8,128)(2,1)} %get-tuple-element.13.high_ref, bf16[1024,1536]{1,0:T(8,128)(2,1)} %get-tuple-element.14.low_ref, f32[12,128]{1,0:T(8,128)} %get-tuple-element.15.scale_ref), custom_call_target="tpu_custom_call" | custom-call | tf_op jit(solution)/shard_map/back/pallas_call | solution.py:486
Async XLA Ops:
  45.3 3.3 %copy-start = (bf16[128,4,1536]{2,1,0:T(4,128)(2,1)S(1)}, bf16[128,4,1536]{2,1,0:T(4,128)(2,1)}, u32[]{:S(2)}) copy-start(bf16[128,4,1536]{2,1,0:T(4,128)(2,1)} %get-tuple-element.10) | copy-start | bytes 4718596

commit v3 on v1

v3 whole, which is shorter than its diff:
```python
import math

import jax
import jax.numpy as jnp
from jax import lax
from jax.experimental import pallas as pl
from jax.experimental.pallas import tpu as pltpu
from jax.sharding import PartitionSpec as P

OUT = 196608
MOMENTUM_DECAY = 0.95
EPSILON = 1e-07
NEWTON_A = 3.4445
NEWTON_B = -4.775
NEWTON_C = 2.0315

BLOCK = 256
NBLK = 4
NPAIR = 10
CHUNK = 512
PACKED = 36 * 128
F32 = jnp.float32
BF16 = jnp.bfloat16
MESH = pl.DeviceIdType.MESH


def place():
    gx = lax.axis_index("gx")
    gy = lax.axis_index("gy")
    return lax.div(gx, 4), lax.rem(gx, 4), lax.div(gy, 2), lax.rem(gy, 2)


def peer_of(where, axis, hop):
    x, z, y, core = where
    if axis == 0:
        x = lax.rem(x + hop, 4)
    elif axis == 1:
        y = lax.rem(y + hop, 4)
    elif axis == 2:
        z = lax.rem(z + hop, 4)
    else:
        core = 1 - core
    return (x * 4 + z, y * 2 + core)


def split(value):
    high = value.astype(BF16)
    return high, (value - high.astype(F32)).astype(BF16)


def mxu(left, right):
    return lax.dot_general(left, right, (((1,), (0,)), ((), ())), preferred_element_type=F32)


def mxu_t(left, right):
    return lax.dot_general(left, right, (((1,), (1,)), ((), ())), preferred_element_type=F32)


def pair_of(slot):
    row = lax.rem(slot, NBLK)
    col = lax.rem(row + lax.div(slot, NBLK), NBLK)
    return row, col


def quarters(slot):
    return ((0, 0), (0, 1), (1, 1)) if slot < NBLK else ((0, 0), (0, 1), (1, 0), (1, 1))


def first_of(slot):
    return 3 * slot if slot < NBLK else 3 * NBLK + 4 * (slot - NBLK)


def gather_kernel(grads_ref, lat_ref, ids_ref, offsets_ref, scales_ref, mom_ref,
                  out_ref, head_ref, scale_ref,
                  own_ref, cols_ref, lats_ref, tlt_ref, moms_ref, heads_ref, high_ref, low_ref, acc_ref,
                  packed_ref, core_ref, half_ref, got1_ref, sum1_ref, got2_ref, sum2_ref, got3_ref,
                  gs, gr, own_sem, ms, hs, a1, b1, a2, b2, a3, b3, a4, b4,
                  cs, cr, s1, r1, s2, r2, s3, r3, s4, r4, s5, r5, s6, r6):
    where = place()
    x, z, y, core = where
    coord = (x, y, z)
    parts, total, rows, chunk = cols_ref.shape
    count = parts * chunk
    width = lat_ref.shape[1]
    tasks = total * rows
    me = lax.axis_index("gx") * 8 + lax.axis_index("gy")
    barrier = pltpu.get_barrier_semaphore()
    hops = (2, 1, 3)

    def device(to):
        return (lax.div(to, 8), lax.rem(to, 8))

    def greet(k, carry):
        to = lax.rem(me + lax.rem(k * 37, total), total)
        pl.semaphore_signal(barrier, inc=1, device_id=device(to), device_id_type=MESH)
        return carry

    lax.fori_loop(1, total, greet, 0)

    loads = []
    for q in range(parts):
        load = pltpu.make_async_copy(mom_ref.at[:, q * chunk : (q + 1) * chunk], moms_ref.at[q], ms.at[q])
        load.start()
        loads.append(load)

    own_ref[:, :width] = lat_ref[...]
    at_row = lax.broadcasted_iota(jnp.int32, (rows, 128), 0)
    at_lane = lax.broadcasted_iota(jnp.int32, (rows, 128), 1)
    ids = jnp.zeros((rows, 128), jnp.int32)
    for r in range(rows):
        ids = jnp.where(at_row == r, ids_ref[r], ids)
    fine = jnp.bitwise_and(ids, 15)
    tail = jnp.where(at_lane == 0, ids - fine, jnp.where(at_lane == 1, fine, 0))
    own_ref[:, width:] = tail.astype(F32).astype(BF16)

    column = me * count + 128 * lax.broadcasted_iota(jnp.int32, scale_ref.shape, 0)
    column = column + lax.broadcasted_iota(jnp.int32, scale_ref.shape, 1)

    def level(t, value):
        return jnp.where(column >= offsets_ref[t], scales_ref[t], value)

    scale_ref[...] = lax.fori_loop(0, offsets_ref.shape[0], level, jnp.zeros(scale_ref.shape, F32))

    pl.semaphore_wait(barrier, total - 1)

    started = []

    def remote(src, dst, ssem, rsem, dev):
        copy = pltpu.make_async_remote_copy(
            src_ref=src, dst_ref=dst, send_sem=ssem, recv_sem=rsem, device_id=dev, device_id_type=MESH)
        copy.start()
        started.append(copy)
        return copy

    def arrived(copies):
        for copy in copies:
            copy.wait_recv()

    keep = pltpu.make_async_copy(own_ref, lats_ref.at[x, z, y, core], own_sem)
    keep.start()
    first = [remote(own_ref, lats_ref.at[x, z, y, core], a1.at[k - 1], b1.at[k - 1], peer_of(where, 1, k)) for k in hops]

    def columns_of(owner, q):
        return grads_ref.at[:, pl.ds(pl.multiple_of(owner * count + q * chunk, 128), chunk)]

    for q in range(parts):
        pltpu.make_async_copy(columns_of(me, q), cols_ref.at[q, me], gr.at[q]).start()

    def send(q, low, high):
        def body(k, carry):
            to = lax.rem(me + lax.rem(k * 37, total), total)
            pltpu.make_async_remote_copy(
                src_ref=columns_of(to, q), dst_ref=cols_ref.at[q, me], send_sem=gs.at[q], recv_sem=gr.at[q],
                device_id=device(to), device_id_type=MESH).start()
            return carry

        lax.fori_loop(low, high, body, 0)

    send(0, 1, 64)
    keep.wait()
    arrived(first)
    part = lats_ref.at[x, z, :, core]
    second = [remote(part, part, a2.at[k - 1], b2.at[k - 1], peer_of(where, 2, k)) for k in hops]
    send(0, 64, total)
    arrived(second)
    part = lats_ref.at[x, :, :, core]
    third = [remote(part, part, a3.at[k - 1], b3.at[k - 1], peer_of(where, 0, k)) for k in hops]
    for q in range(1, parts):
        send(q, 1, total)
    arrived(third)
    part = lats_ref.at[:, :, :, core]
    arrived([remote(part, part, a4, b4, peer_of(where, 3, 1))])

    def flat(value):
        value = value.astype(F32).reshape(total // 2, 2, rows, value.shape[-1])
        return jnp.concatenate([value[:, 0], value[:, 1]], axis=1).reshape(tasks, value.shape[-1])

    lat = flat(lats_ref[...].reshape(total, rows, width + 128))
    task = jnp.sum(lat[:, width:], axis=1, keepdims=True)
    which = lax.broadcasted_iota(jnp.int32, (tasks, tasks), 1).astype(F32)
    onehot = jnp.where(which == task, 1.0, 0.0).astype(BF16)
    tlt_ref[...] = mxu(onehot, lat[:, :width].astype(BF16)).T.astype(BF16)
    acc_ref[...] = jnp.zeros_like(acc_ref)

    def gram(low, high):
        def body(slot, carry):
            row, col = pair_of(slot)
            top = pl.ds(pl.multiple_of(row * BLOCK, BLOCK), BLOCK)
            side = pl.ds(pl.multiple_of(col * BLOCK, BLOCK), BLOCK)
            acc_ref[slot] += (
                mxu_t(high_ref[top, :], high_ref[side, :])
                + mxu_t(high_ref[top, :], low_ref[side, :])
                + mxu_t(low_ref[top, :], high_ref[side, :])
            )
            return carry

        lax.fori_loop(low, high, body, 0)

    def blend(q):
        pltpu.make_async_copy(cols_ref.at[q], cols_ref.at[q], gr.at[q]).wait()
        loads[q].wait()
        cols = flat(cols_ref[q]).astype(BF16)
        for i in range(NBLK):
            at = slice(i * BLOCK, (i + 1) * BLOCK)
            head = mxu(tlt_ref[at, :], cols)
            heads_ref[q, at, :] = head
            new_momentum = MOMENTUM_DECAY * moms_ref[q, at, :] + head
            high, low = split(head + MOMENTUM_DECAY * new_momentum)
            high_ref[at, :] = high
            low_ref[at, :] = low
        store = pltpu.make_async_copy(heads_ref.at[q], head_ref.at[:, q * chunk : (q + 1) * chunk], hs.at[q])
        store.start()
        return store

    stores = []
    for q in range(parts - 1):
        stores.append(blend(q))
        gram(0, NPAIR)
    stores.append(blend(parts - 1))

    other = 1 - core
    size = packed_ref.shape[1]
    halfs, quart, piece = size // 2, size // 8, size // 32

    def span(index, length):
        return pl.ds(pl.multiple_of(index * length, 8), length)

    cored = []
    edges = (0, NBLK, NBLK + 3, NPAIR)
    for r in range(3):
        gram(edges[r], edges[r + 1])
        for slot in range(edges[r], edges[r + 1]):
            small = BLOCK // 2
            for at, (i, j) in enumerate(quarters(slot)):
                base = (first_of(slot) + at) * small - r * size
                packed_ref[r, base : base + small, :] = acc_ref[slot, i * small : (i + 1) * small, j * small : (j + 1) * small]
        cored.append(remote(packed_ref.at[r, span(other, halfs)], core_ref.at[r], cs.at[r], cr.at[r], peer_of(where, 3, 1)))

    phase = []
    for r in range(3):
        cored[r].wait_recv()
        half_ref[r] = packed_ref[r, span(core, halfs), :] + core_ref[r]
        phase.append([
            remote(half_ref.at[r, span(lax.rem(coord[r] + k, 4), quart)], got1_ref.at[r, k - 1],
                   s1.at[r, k - 1], r1.at[r, k - 1], peer_of(where, r, k)) for k in hops])
    phase2 = []
    for r in range(3):
        b = (r + 1) % 3
        arrived(phase[r])
        sum1_ref[r] = (half_ref[r, span(coord[r], quart), :] + got1_ref[r, 0]) + (got1_ref[r, 1] + got1_ref[r, 2])
        phase2.append([
            remote(sum1_ref.at[r, span(lax.rem(coord[b] + k, 4), piece)], got2_ref.at[r, k - 1],
                   s2.at[r, k - 1], r2.at[r, k - 1], peer_of(where, b, k)) for k in hops])
    phase3 = []
    for r in range(3):
        b, d = (r + 1) % 3, (r + 2) % 3
        arrived(phase2[r])
        sum2_ref[r] = (sum1_ref[r, span(coord[b], piece), :] + got2_ref[r, 0]) + (got2_ref[r, 1] + got2_ref[r, 2])
        phase3.append([
            remote(sum2_ref.at[r], got3_ref.at[r, k - 1], s3.at[r, k - 1], r3.at[r, k - 1], peer_of(where, d, k))
            for k in hops])
    phase4 = []
    for r in range(3):
        b = (r + 1) % 3
        arrived(phase3[r])
        mine = span(core * 16 + coord[r] * 4 + coord[b], piece)
        out_ref[r, mine, :] = (sum2_ref[r] + got3_ref[r, 0]) + (got3_ref[r, 1] + got3_ref[r, 2])
        own = out_ref.at[r, mine]
        phase4.append([remote(own, own, s4.at[r, k - 1], r4.at[r, k - 1], peer_of(where, b, k)) for k in hops])
    phase5 = []
    for r in range(3):
        arrived(phase4[r])
        own = out_ref.at[r, span(core * 4 + coord[r], quart)]
        phase5.append([remote(own, own, s5.at[r, k - 1], r5.at[r, k - 1], peer_of(where, r, k)) for k in hops])
    last = []
    for r in range(3):
        arrived(phase5[r])
        own = out_ref.at[r, span(core, halfs)]
        last.append(remote(own, own, s6.at[r], r6.at[r], peer_of(where, 3, 1)))
    arrived(last)
    for copy in started:
        copy.wait_send()
    for q in range(parts):
        sent = cols_ref.at[q, pl.ds(0, total - 1)]
        pltpu.make_async_copy(sent, sent, gs.at[q]).wait()
        stores[q].wait()


def gather(grads, lat, ids, offsets, scales, momentum):
    rows, latent = lat.shape
    width, count = momentum.shape
    total = grads.shape[1] // count
    parts = count // CHUNK
    tasks = rows * total
    size = PACKED // 3
    dma = pltpu.SemaphoreType.DMA
    smem = pl.BlockSpec(memory_space=pltpu.SMEM)
    vmem = pl.BlockSpec(memory_space=pltpu.VMEM)
    anywhere = pl.BlockSpec(memory_space=pl.ANY)
    return pl.pallas_call(
        gather_kernel,
        in_specs=[anywhere, vmem, smem, smem, smem, anywhere],
        out_specs=[vmem, anywhere, vmem],
        out_shape=[
            jax.ShapeDtypeStruct((3, size, 128), F32),
            jax.ShapeDtypeStruct((width, count), F32),
            jax.ShapeDtypeStruct((count // 128, 128), F32),
        ],
        scratch_shapes=[
            pltpu.VMEM((rows, latent + 128), BF16),
            pltpu.VMEM((parts, total, rows, CHUNK), BF16),
            pltpu.VMEM((4, 4, 4, 2, rows, latent + 128), BF16),
            pltpu.VMEM((width, tasks), BF16),
            pltpu.VMEM((parts, width, CHUNK), F32),
            pltpu.VMEM((parts, width, CHUNK), F32),
            pltpu.VMEM((width, CHUNK), BF16),
            pltpu.VMEM((width, CHUNK), BF16),
            pltpu.VMEM((NPAIR, BLOCK, BLOCK), F32),
            pltpu.VMEM((3, size, 128), F32),
            pltpu.VMEM((3, size // 2, 128), F32),
            pltpu.VMEM((3, size // 2, 128), F32),
            pltpu.VMEM((3, 3, size // 8, 128), F32),
            pltpu.VMEM((3, size // 8, 128), F32),
            pltpu.VMEM((3, 3, size // 32, 128), F32),
            pltpu.VMEM((3, size // 32, 128), F32),
            pltpu.VMEM((3, 3, size // 32, 128), F32),
            dma((parts,)), dma((parts,)), dma, dma((parts,)), dma((parts,)),
        ]
        + [dma((3,))] * 6 + [dma, dma, dma((3,)), dma((3,))]
        + [dma((3, 3))] * 10 + [dma((3,)), dma((3,))],
        compiler_params=pltpu.CompilerParams(collective_id=1, has_side_effects=True, vmem_limit_bytes=60 << 20),
        name="gather",
    )(grads, lat, ids, offsets, scales, momentum)


def back_kernel(gram_ref, head_ref, mom_ref, scale_ref, newmom_ref, step_ref, inv_ref, mats_ref, high_ref, low_ref):
    G, M1, T, G2 = 0, 1, 2, 3

    def unpack(slot):
        half = BLOCK // 2
        base = first_of(slot) * half
        part = [gram_ref[base + at * half : base + (at + 1) * half, :] for at in range(len(quarters(slot)))]
        if slot < NBLK:
            part = [part[0], part[1], part[1].T, part[2]]
        top = jnp.concatenate(part[:2], axis=1)
        return jnp.concatenate([top, jnp.concatenate(part[2:], axis=1)], axis=0)

    def store(which, row, col, value):
        high, low = split(value)
        rows = pl.ds(pl.multiple_of(row * BLOCK, BLOCK), BLOCK)
        cols = pl.ds(pl.multiple_of(col * BLOCK, BLOCK), BLOCK)
        mats_ref[which, 0, col, rows, :] = high
        mats_ref[which, 1, col, rows, :] = low
        flipped, flipped_low = split(value.T)
        mats_ref[which, 0, row, cols, :] = flipped
        mats_ref[which, 1, row, cols, :] = flipped_low

    def eye(row, col):
        r = lax.broadcasted_iota(jnp.int32, (BLOCK, BLOCK), 0)
        c = lax.broadcasted_iota(jnp.int32, (BLOCK, BLOCK), 1)
        return jnp.where((r == c) & (row == col), 1.0, 0.0)

    def product(left, right, row, col):
        rows = pl.ds(pl.multiple_of(row * BLOCK, BLOCK), BLOCK)
        total = None
        for k in range(NBLK):
            ks = slice(k * BLOCK, (k + 1) * BLOCK)
            lh, ll = mats_ref[left, 0, k, rows, :], mats_ref[left, 1, k, rows, :]
            rh, rl = mats_ref[right, 0, col, ks, :], mats_ref[right, 1, col, ks, :]
            term = mxu(lh, rh) + mxu(lh, rl) + mxu(ll, rh)
            total = term if total is None else total + term
        return total

    def stage(left, right, dest, finish):
        def body(slot, carry):
            row, col = pair_of(slot)
            store(dest, row, col, finish(slot, row, col, product(left, right, row, col)))
            return carry

        lax.fori_loop(0, NPAIR, body, 0)

    @pl.when(pl.program_id(0) == 0)
    def _():
        r = lax.broadcasted_iota(jnp.int32, (BLOCK, BLOCK), 0)
        c = lax.broadcasted_iota(jnp.int32, (BLOCK, BLOCK), 1)
        diagonal = unpack(0) + unpack(1) + unpack(2) + unpack(3)
        picked = jnp.where(r == c, diagonal, 0.0)
        squares = jnp.sum(jnp.sum(picked, axis=1, keepdims=True), axis=0, keepdims=True)
        inverse = 1.0 / (jnp.sqrt(squares) + EPSILON)
        inv_ref[...] = jnp.broadcast_to(inverse, inv_ref.shape)

        for slot in range(NPAIR):
            row = slot % NBLK
            store(G, row, (row + slot // NBLK) % NBLK, (unpack(slot) * inverse) * inverse)

        def newton(which):
            def finish(slot, row, col, value):
                rows = pl.ds(pl.multiple_of(row * BLOCK, BLOCK), BLOCK)
                own = mats_ref[which, 0, col, rows, :].astype(F32) + mats_ref[which, 1, col, rows, :].astype(F32)
                return NEWTON_A * eye(row, col) + NEWTON_B * own + NEWTON_C * value

            return finish

        plain = lambda slot, row, col, value: value
        stage(G, G, M1, newton(G))
        stage(G, M1, T, plain)
        stage(T, M1, G2, plain)
        stage(G2, G2, G, newton(G2))
        stage(G, M1, T, plain)

    new_momentum = MOMENTUM_DECAY * mom_ref[...] + head_ref[...]
    newmom_ref[...] = new_momentum
    high_ref[...], low_ref[...] = split(head_ref[...] + MOMENTUM_DECAY * new_momentum)
    width = CHUNK // 128
    factor = [
        scale_ref[pl.ds(pl.program_id(0) * width + at, 1), :] * (math.sqrt(OUT) * inv_ref[0:1, 0:1])
        for at in range(width)
    ]
    for i in range(NBLK):
        rows = slice(i * BLOCK, (i + 1) * BLOCK)
        total = None
        for k in range(NBLK):
            ks = slice(k * BLOCK, (k + 1) * BLOCK)
            mh, ml = mats_ref[T, 0, k, rows, :], mats_ref[T, 1, k, rows, :]
            term = mxu(mh, high_ref[ks, :]) + mxu(mh, low_ref[ks, :]) + mxu(ml, high_ref[ks, :])
            total = term if total is None else total + term
        for at in range(width):
            lanes = slice(at * 128, (at + 1) * 128)
            step_ref[rows, lanes] = total[:, lanes] * factor[at]


def back(gram, head, momentum, scale):
    width, count = head.shape
    return pl.pallas_call(
        back_kernel,
        grid=(count // CHUNK,),
        in_specs=[
            pl.BlockSpec(gram.shape, lambda c: (0, 0)),
            pl.BlockSpec((width, CHUNK), lambda c: (0, c)),
            pl.BlockSpec((width, CHUNK), lambda c: (0, c)),
            pl.BlockSpec(scale.shape, lambda c: (0, 0)),
        ],
        out_specs=[pl.BlockSpec((width, CHUNK), lambda c: (0, c))] * 2,
        out_shape=[jax.ShapeDtypeStruct((width, count), F32)] * 2,
        scratch_shapes=[
            pltpu.VMEM((8, 128), F32),
            pltpu.VMEM((4, 2, NBLK, width, BLOCK), BF16),
            pltpu.VMEM((width, CHUNK), BF16),
            pltpu.VMEM((width, CHUNK), BF16),
        ],
        compiler_params=pltpu.CompilerParams(vmem_limit_bytes=60 << 20),
        name="back",
    )(gram, head, momentum, scale)


def per_device(factor_grads, latents, task_ids, offsets, target_scale, momentum):
    gram, head, column_scale = gather(factor_grads, latents, task_ids, offsets, target_scale, momentum)
    new_momentum, step = back(gram.reshape(-1, 128), head, momentum, column_scale)
    return new_momentum, step


def solution(mesh):
    placed = (
        P(("gx", "gy"), None),
        P(("gx", "gy"), None),
        P(("gx", "gy")),
        P(),
        P(),
        P(None, ("gx", "gy")),
    )
    return jax.shard_map(
        per_device,
        mesh=mesh,
        in_specs=placed,
        out_specs=(P(None, ("gx", "gy")), P(None, ("gx", "gy"))),
        check_vma=False,
    )
```

time: 317 us -> 129 us (0.41)
  waiting for transfers between devices: 189 us -> 0 us
  Pallas kernels: 69.5 us -> 128 us
  blocking collectives: 36.2 us -> 0 us
  between operations: 14.1 us -> 0.64 us
  local copies, waits for them, and re-layouts: 5.85 us -> 0 us
    psum x1 -> x0, waiting for transfers between devices: 148 us -> none  [per_device(): gram = lax.psum(gram, axes)]
    pallas_call x1, Pallas kernels: 20.6 us -> 79.7 us  [gather(): pl.pallas_call(gather_kernel, in_specs=[anywhere, vmem, smem, smem, smem,...]
    all_gather x1 -> x0, waiting for transfers between devices: 41.2 us -> none  [per_device(): lax.all_gather(jnp.concatenate([latents, tail], axis=1), axes, axis=0, ti...]
    all_to_all x1 -> x0, blocking collectives: 36.2 us -> none  [per_device(): lax.all_to_all(factor_grads, axes, split_axis=1, concat_axis=0, tiled=True)]
    unnamed x6 -> x0, local copies, waits for them, and re-layouts: 3.87 us -> none
  transfers between devices with their start and end apart: 2 -> 0, of which waited for: 2 -> 0; matrix products, arithmetic and copies ran while one was open for 0% -> 0% of each run, Pallas kernels for 0% -> 0%
where the time goes in v3:
time: 129 us
  Pallas kernels  128 us (99%)
    pallas_call x1, Pallas kernels, gather(): pl.pallas_call(gather_kernel, in_specs=[anywhere, vmem, smem, smem, smem,...  79.7 us
    pallas_call x1, Pallas kernels, back(): pl.pallas_call(back_kernel, grid=(count // CHUNK,), in_specs=[pl.BlockSpe...  48.8 us

profile of v3, /device:TPU:1, one launch (start us, length us, event | category | flops | bytes accessed | tf_op | source)
XLA Modules:
  0.0 129.1 jit_solution(14102014834283913533)
XLA Ops:
  0.6 79.7 %gather.1 = (f32[3,1536,128]{2,1,0:T(8,128)}, f32[1024,1536]{1,0:T(8,128)}, f32[12,128]{1,0:T(8,128)}) custom-call(bf16[4,196608]{1,0:T(4,128)(2,1)} %grads_ref.1, bf16[4,1024]{1,0:T(4,128)(2,1)} %lat_ref.1, s32[4]{0:T(128)} %ids_ref.1, s32[160]{0:T(256)} %offsets_ref.1, f32[160]{0:T(256)} %scales_ref.1, f32[1024,1536]{1,0:T(8,128)} %mom_ref.3), custom_call_target="tpu_custom_call" | custom-call | tf_op jit(solution)/shard_map/gather/pallas_call | solution.py:300
  80.3 48.8 %back.1 = (f32[1024,1536]{1,0:T(8,128)}, f32[1024,1536]{1,0:T(8,128)}) custom-call(f32[4608,128]{1,0:T(8,128)} %bitcast.1, f32[1024,1536]{1,0:T(8,128)} %get-tuple-element.6.head_ref, f32[1024,1536]{1,0:T(8,128)} %mom_ref.3, f32[12,128]{1,0:T(8,128)} %get-tuple-element.7.scale_ref), custom_call_target="tpu_custom_call" | custom-call | tf_op jit(solution)/shard_map/back/pallas_call | solution.py:434

commit v4 on v3

v4 whole, which is shorter than its diff:
```python
import math

import jax
import jax.numpy as jnp
from jax import lax
from jax.experimental import pallas as pl
from jax.experimental.pallas import tpu as pltpu
from jax.sharding import PartitionSpec as P

OUT = 196608
MOMENTUM_DECAY = 0.95
EPSILON = 1e-07
NEWTON_A = 3.4445
NEWTON_B = -4.775
NEWTON_C = 2.0315

BLOCK = 256
NBLK = 4
NPAIR = 10
CHUNK = 512
WIDTHS = (512, 512, 512)
PACKED = 36 * 128
F32 = jnp.float32
BF16 = jnp.bfloat16
MESH = pl.DeviceIdType.MESH


def place():
    gx = lax.axis_index("gx")
    gy = lax.axis_index("gy")
    return lax.div(gx, 4), lax.rem(gx, 4), lax.div(gy, 2), lax.rem(gy, 2)


def peer_of(where, axis, hop):
    x, z, y, core = where
    if axis == 0:
        x = lax.rem(x + hop, 4)
    elif axis == 1:
        y = lax.rem(y + hop, 4)
    elif axis == 2:
        z = lax.rem(z + hop, 4)
    else:
        core = 1 - core
    return (x * 4 + z, y * 2 + core)


def split(value):
    high = value.astype(BF16)
    return high, (value - high.astype(F32)).astype(BF16)


def mxu(left, right):
    return lax.dot_general(left, right, (((1,), (0,)), ((), ())), preferred_element_type=F32)


def mxu_t(left, right):
    return lax.dot_general(left, right, (((1,), (1,)), ((), ())), preferred_element_type=F32)


def pair_of(slot):
    row = lax.rem(slot, NBLK)
    col = lax.rem(row + lax.div(slot, NBLK), NBLK)
    return row, col


def gather_kernel(grads_ref, lat_ref, ids_ref, offsets_ref, scales_ref, mom_ref,
                  final_ref, head_ref, scale_ref,
                  own_ref, cols_refs, lats_ref, tlt_ref, moms_ref, heads_ref, high_ref, low_ref, acc_ref,
                  packed_ref, core_ref, half_ref, got1_ref, sum1_ref, got2_ref, sum2_ref, got3_ref,
                  sums_ref, mats_ref, trace_ref,
                  gs, gr, own_sem, ms, hs, a1, b1, a2, b2, a3, b3, a4, b4,
                  cs, cr, s1, r1, s2, r2, s3, r3, s4, r4, s5, r5, ts, tr, ps, pr):
    where = place()
    x, z, y, core = where
    coord = (x, y, z)
    parts = len(cols_refs)
    total, rows = cols_refs[0].shape[:2]
    widths = [ref.shape[2] for ref in cols_refs]
    begin = [sum(widths[:q]) for q in range(parts)]
    count = sum(widths)
    width = lat_ref.shape[1]
    tasks = total * rows
    me = lax.axis_index("gx") * 8 + lax.axis_index("gy")
    barrier = pltpu.get_barrier_semaphore()
    hops = (2, 1, 3)

    def device(to):
        return (lax.div(to, 8), lax.rem(to, 8))

    def greet(k, carry):
        to = lax.rem(me + lax.rem(k * 37, total), total)
        pl.semaphore_signal(barrier, inc=1, device_id=device(to), device_id_type=MESH)
        return carry

    lax.fori_loop(1, total, greet, 0)

    loads = []
    for q in range(parts):
        lanes = slice(begin[q], begin[q] + widths[q])
        load = pltpu.make_async_copy(mom_ref.at[:, lanes], moms_ref.at[:, lanes], ms.at[q])
        load.start()
        loads.append(load)

    own_ref[:, :width] = lat_ref[...]
    at_row = lax.broadcasted_iota(jnp.int32, (rows, 128), 0)
    at_lane = lax.broadcasted_iota(jnp.int32, (rows, 128), 1)
    ids = jnp.zeros((rows, 128), jnp.int32)
    for r in range(rows):
        ids = jnp.where(at_row == r, ids_ref[r], ids)
    fine = jnp.bitwise_and(ids, 15)
    tail = jnp.where(at_lane == 0, ids - fine, jnp.where(at_lane == 1, fine, 0))
    own_ref[:, width:] = tail.astype(F32).astype(BF16)

    column = me * count + 128 * lax.broadcasted_iota(jnp.int32, scale_ref.shape, 0)
    column = column + lax.broadcasted_iota(jnp.int32, scale_ref.shape, 1)

    def level(t, value):
        return jnp.where(column >= offsets_ref[t], scales_ref[t], value)

    scale_ref[...] = lax.fori_loop(0, offsets_ref.shape[0], level, jnp.zeros(scale_ref.shape, F32))

    pl.semaphore_wait(barrier, total - 1)

    started = []

    def remote(src, dst, ssem, rsem, dev):
        copy = pltpu.make_async_remote_copy(
            src_ref=src, dst_ref=dst, send_sem=ssem, recv_sem=rsem, device_id=dev, device_id_type=MESH)
        copy.start()
        started.append(copy)
        return copy

    def arrived(copies):
        for copy in copies:
            copy.wait_recv()

    keep = pltpu.make_async_copy(own_ref, lats_ref.at[x, z, y, core], own_sem)
    keep.start()
    third = (width + 128) // 3
    orders = ((1, 2, 0), (2, 0, 1), (0, 1, 2))

    def region(p, level):
        full = orders[p][:level]
        at = tuple(slice(None) if axis in full else coord[axis] for axis in (0, 2, 1))
        return lats_ref.at[at + (core, slice(None), slice(p * third, (p + 1) * third))]

    def spread(level, ssem, rsem):
        copies = []
        for p in range(3):
            source = own_ref.at[:, p * third : (p + 1) * third] if level == 0 else region(p, level)
            for k in hops:
                copies.append(remote(source, region(p, level), ssem.at[p, k - 1], rsem.at[p, k - 1],
                                     peer_of(where, orders[p][level], k)))
        return copies

    first = spread(0, a1, b1)

    def columns_of(owner, q):
        return grads_ref.at[:, pl.ds(pl.multiple_of(owner * count + begin[q], 128), widths[q])]

    for q in range(parts):
        pltpu.make_async_copy(columns_of(me, q), cols_refs[q].at[me], gr.at[q]).start()

    def send(q, low, high):
        def body(k, carry):
            to = lax.rem(me + lax.rem(k * 37, total), total)
            pltpu.make_async_remote_copy(
                src_ref=columns_of(to, q), dst_ref=cols_refs[q].at[me], send_sem=gs.at[q], recv_sem=gr.at[q],
                device_id=device(to), device_id_type=MESH).start()
            return carry

        lax.fori_loop(low, high, body, 0)

    send(0, 1, 48)
    keep.wait()
    arrived(first)
    second = spread(1, a2, b2)
    send(0, 48, 88)
    arrived(second)
    rest = spread(2, a3, b3)
    send(0, 88, total)
    for q in range(1, parts):
        send(q, 1, total)
    arrived(rest)
    part = lats_ref.at[:, :, :, core]
    arrived([remote(part, part, a4, b4, peer_of(where, 3, 1))])

    def flat(value):
        value = value.astype(F32).reshape(total // 2, 2, rows, value.shape[-1])
        return jnp.concatenate([value[:, 0], value[:, 1]], axis=1).reshape(tasks, value.shape[-1])

    lat = flat(lats_ref[...].reshape(total, rows, width + 128))
    task = jnp.sum(lat[:, width:], axis=1, keepdims=True)
    which = lax.broadcasted_iota(jnp.int32, (tasks, tasks), 1).astype(F32)
    onehot = jnp.where(which == task, 1.0, 0.0).astype(BF16)
    tlt_ref[...] = mxu(onehot, lat[:, :width].astype(BF16)).T.astype(BF16)
    acc_ref[...] = jnp.zeros_like(acc_ref)

    def gram(used, low, high):
        def body(slot, carry):
            row, col = pair_of(slot)
            top = pl.ds(pl.multiple_of(row * BLOCK, BLOCK), BLOCK)
            side = pl.ds(pl.multiple_of(col * BLOCK, BLOCK), BLOCK)
            acc_ref[slot] += (
                mxu_t(high_ref[top, :used], high_ref[side, :used])
                + mxu_t(high_ref[top, :used], low_ref[side, :used])
                + mxu_t(low_ref[top, :used], high_ref[side, :used])
            )
            return carry

        lax.fori_loop(low, high, body, 0)

    def blend(q):
        pltpu.make_async_copy(cols_refs[q], cols_refs[q], gr.at[q]).wait()
        loads[q].wait()
        cols = flat(cols_refs[q][...]).astype(BF16)
        lanes = slice(begin[q], begin[q] + widths[q])
        for i in range(NBLK):
            at = slice(i * BLOCK, (i + 1) * BLOCK)
            head = mxu(tlt_ref[at, :], cols)
            heads_ref[at, lanes] = head
            new_momentum = MOMENTUM_DECAY * moms_ref[at, lanes] + head
            high, low = split(head + MOMENTUM_DECAY * new_momentum)
            high_ref[at, : widths[q]] = high
            low_ref[at, : widths[q]] = low
        store = pltpu.make_async_copy(heads_ref.at[:, lanes], head_ref.at[:, lanes], hs.at[q])
        store.start()
        return store

    stores = []
    for q in range(parts - 1):
        stores.append(blend(q))
        gram(widths[q], 0, NPAIR)
    stores.append(blend(parts - 1))

    other = 1 - core
    size = packed_ref.shape[1]
    halfs, quart, piece = size // 2, size // 8, size // 32
    small = BLOCK // 2

    def span(index, length):
        return pl.ds(pl.multiple_of(index * length, 8), length)

    cored = []
    groups = (((0, 4),), ((4, 6), (7, 9)), ((6, 7), (9, 10)))
    every = tuple((i, j) for i in range(2) for j in range(2))
    layout = (
        tuple((slot, q) for slot in range(NBLK) for q in ((0, 0), (0, 1), (1, 1))),
        tuple((4, q) for q in every) + tuple((5, q) for q in every[:2])
        + tuple((7, q) for q in every) + tuple((8, q) for q in every[:2]),
        tuple((6, q) for q in every) + tuple((5, q) for q in every[2:])
        + tuple((9, q) for q in every) + tuple((8, q) for q in every[2:]),
    )
    for r in range(3):
        for low, high in groups[r]:
            gram(widths[-1], low, high)
        for at, (slot, (i, j)) in enumerate(layout[r]):
            packed_ref[r, at * small : (at + 1) * small, :] = acc_ref[slot, i * small : (i + 1) * small, j * small : (j + 1) * small]
        cored.append(remote(packed_ref.at[r, span(other, halfs)], core_ref.at[r], cs.at[r], cr.at[r], peer_of(where, 3, 1)))

    phase = []
    for r in range(3):
        cored[r].wait_recv()
        half_ref[r] = packed_ref[r, span(core, halfs), :] + core_ref[r]
        phase.append([
            remote(half_ref.at[r, span(lax.rem(coord[r] + k, 4), quart)], got1_ref.at[r, k - 1],
                   s1.at[r, k - 1], r1.at[r, k - 1], peer_of(where, r, k)) for k in hops])
    phase2 = []
    for r in range(3):
        b = (r + 1) % 3
        arrived(phase[r])
        sum1_ref[r] = (half_ref[r, span(coord[r], quart), :] + got1_ref[r, 0]) + (got1_ref[r, 1] + got1_ref[r, 2])
        phase2.append([
            remote(sum1_ref.at[r, span(lax.rem(coord[b] + k, 4), piece)], got2_ref.at[r, k - 1],
                   s2.at[r, k - 1], r2.at[r, k - 1], peer_of(where, b, k)) for k in hops])
    phase3 = []
    for r in range(3):
        b, d = (r + 1) % 3, (r + 2) % 3
        arrived(phase2[r])
        sum2_ref[r] = (sum1_ref[r, span(coord[b], piece), :] + got2_ref[r, 0]) + (got2_ref[r, 1] + got2_ref[r, 2])
        phase3.append([
            remote(sum2_ref.at[r], got3_ref.at[r, k - 1], s3.at[r, k - 1], r3.at[r, k - 1], peer_of(where, d, k))
            for k in hops])
    phase4 = []
    for r in range(3):
        b = (r + 1) % 3
        arrived(phase3[r])
        mine = span(coord[r] * 4 + coord[b], piece)
        sums_ref[r, mine, :] = (sum2_ref[r] + got3_ref[r, 0]) + (got3_ref[r, 1] + got3_ref[r, 2])
        own = sums_ref.at[r, mine]
        phase4.append([remote(own, own, s4.at[r, k - 1], r4.at[r, k - 1], peer_of(where, b, k)) for k in hops])
    phase5 = []
    for r in range(3):
        arrived(phase4[r])
        own = sums_ref.at[r, span(coord[r], quart)]
        phase5.append([remote(own, own, s5.at[r, k - 1], r5.at[r, k - 1], peer_of(where, r, k)) for k in hops])

    G, M1, T, G2, M2 = range(5)
    partner = peer_of(where, 3, 1)
    final = 5

    def tile(which, part, row, col):
        rows_at = pl.ds(pl.multiple_of(row * BLOCK, BLOCK), BLOCK)
        if which == final:
            return final_ref.at[part, col, rows_at, :]
        return mats_ref.at[which, part, col, rows_at, :]

    def store(which, row, col, value, mirrored):
        values = list(split(value))
        tiles = [tile(which, 0, row, col), tile(which, 1, row, col)]
        if mirrored:
            values += list(split(value.T))
            tiles += [tile(which, 0, col, row), tile(which, 1, col, row)]
        for at, block in zip(tiles, values):
            at[...] = block
        for at in tiles:
            pltpu.make_async_remote_copy(
                src_ref=at, dst_ref=at, send_sem=ps.at[which], recv_sem=pr.at[which],
                device_id=partner, device_id_type=MESH).start()

    def finished(which):
        one = final_ref.at[0] if which == final else mats_ref.at[which, 0]
        pltpu.make_async_copy(one, one, pr.at[which]).wait()

    def diagonal(t):
        slot = 2 * core + t
        return slot, slot

    def beside(t):
        return pair_of(4 + 3 * core + t)

    def block(r, at):
        return sums_ref[r, at * small : (at + 1) * small, :]

    def square(parts4):
        top = jnp.concatenate(parts4[:2], axis=1)
        return jnp.concatenate([top, jnp.concatenate(parts4[2:], axis=1)], axis=0)

    arrived(phase5[0])
    r_at = lax.broadcasted_iota(jnp.int32, (small, small), 0)
    c_at = lax.broadcasted_iota(jnp.int32, (small, small), 1)
    squares = jnp.where(r_at == c_at, (block(0, 0) + block(0, 2)) + (block(0, 3) + block(0, 5)), 0.0)
    squares = jnp.sum(jnp.sum(squares, axis=1, keepdims=True), axis=0, keepdims=True)
    trace_ref[0] = jnp.broadcast_to(squares, trace_ref.shape[1:])
    traced = remote(trace_ref.at[0], trace_ref.at[1], ts, tr, partner)
    for t in range(2):
        value = square([block(0, 3 * t), block(0, 3 * t + 1), block(0, 3 * t + 1).T, block(0, 3 * t + 2)])
        store(G, *diagonal(t), value, False)
    arrived(phase5[1])
    store(G, *beside(0), square([block(1, at) for at in range(4)]), True)
    arrived(phase5[2])
    store(G, *beside(1), square([block(1, 4), block(1, 5), block(2, 4), block(2, 5)]), True)
    store(G, *beside(2), square([block(2, at) for at in range(4)]), True)
    arrived([traced])
    inverse = 1.0 / (jnp.sqrt(trace_ref[0, 0:1, 0:1] + trace_ref[1, 0:1, 0:1]) + EPSILON)
    trace_ref[2] = jnp.broadcast_to(inverse, trace_ref.shape[1:])
    scale_ref[...] = scale_ref[...] * (math.sqrt(OUT) * inverse)
    finished(G)

    def eye(row, col):
        i = lax.broadcasted_iota(jnp.int32, (BLOCK, BLOCK), 0)
        j = lax.broadcasted_iota(jnp.int32, (BLOCK, BLOCK), 1)
        return jnp.where((i == j) & (row == col), 1.0, 0.0)

    def product(left, right, row, col):
        total_block = None
        for k in range(NBLK):
            lh, ll = tile(left, 0, row, k)[...], tile(left, 1, row, k)[...]
            rh, rl = tile(right, 0, k, col)[...], tile(right, 1, k, col)[...]
            term = mxu(lh, rh) + mxu(lh, rl) + mxu(ll, rh)
            total_block = term if total_block is None else total_block + term
        return total_block

    def stage(left, right, dest, finish):
        def off(t, carry):
            row, col = beside(t)
            store(dest, row, col, finish(row, col, product(left, right, row, col)), True)
            return carry

        def on(t, carry):
            row, col = diagonal(t)
            store(dest, row, col, finish(row, col, product(left, right, row, col)), False)
            return carry

        lax.fori_loop(0, 3, off, 0)
        lax.fori_loop(0, 2, on, 0)
        finished(dest)

    def newton(which, scaled):
        def finish(row, col, value):
            own = tile(which, 0, row, col)[...].astype(F32) + tile(which, 1, row, col)[...].astype(F32)
            if scaled:
                inv = trace_ref[2, 0:1, 0:1]
                own = (own * inv) * inv
                value = (((value * inv) * inv) * inv) * inv
            return NEWTON_A * eye(row, col) + NEWTON_B * own + NEWTON_C * value

        return finish

    def normal(row, col, value):
        inv = trace_ref[2, 0:1, 0:1]
        return (value * inv) * inv

    plain = lambda row, col, value: value
    stage(G, G, M1, newton(G, True))
    stage(G, M1, T, normal)
    stage(T, M1, G2, plain)
    stage(G2, G2, M2, newton(G2, False))
    stage(M2, M1, final, plain)
    for copy in started:
        copy.wait_send()
    for which in range(6):
        one = mats_ref.at[0, 0]
        pltpu.make_async_copy(one, one, ps.at[which]).wait()
    for q in range(parts):
        sent = cols_refs[q].at[pl.ds(0, total - 1)]
        pltpu.make_async_copy(sent, sent, gs.at[q]).wait()
        stores[q].wait()


def gather(grads, lat, ids, offsets, scales, momentum):
    rows, latent = lat.shape
    width, count = momentum.shape
    total = grads.shape[1] // count
    parts = len(WIDTHS)
    tasks = rows * total
    size = PACKED // 3
    dma = pltpu.SemaphoreType.DMA
    smem = pl.BlockSpec(memory_space=pltpu.SMEM)
    vmem = pl.BlockSpec(memory_space=pltpu.VMEM)
    anywhere = pl.BlockSpec(memory_space=pl.ANY)
    return pl.pallas_call(
        gather_kernel,
        in_specs=[anywhere, vmem, smem, smem, smem, anywhere],
        out_specs=[vmem, anywhere, vmem],
        out_shape=[
            jax.ShapeDtypeStruct((2, NBLK, width, BLOCK), BF16),
            jax.ShapeDtypeStruct((width, count), F32),
            jax.ShapeDtypeStruct((count // 128, 128), F32),
        ],
        scratch_shapes=[
            pltpu.VMEM((rows, latent + 128), BF16),
            [pltpu.VMEM((total, rows, wide), BF16) for wide in WIDTHS],
            pltpu.VMEM((4, 4, 4, 2, rows, latent + 128), BF16),
            pltpu.VMEM((width, tasks), BF16),
            pltpu.VMEM((width, count), F32),
            pltpu.VMEM((width, count), F32),
            pltpu.VMEM((width, max(WIDTHS)), BF16),
            pltpu.VMEM((width, max(WIDTHS)), BF16),
            pltpu.VMEM((NPAIR, BLOCK, BLOCK), F32),
            pltpu.VMEM((3, size, 128), F32),
            pltpu.VMEM((3, size // 2, 128), F32),
            pltpu.VMEM((3, size // 2, 128), F32),
            pltpu.VMEM((3, 3, size // 8, 128), F32),
            pltpu.VMEM((3, size // 8, 128), F32),
            pltpu.VMEM((3, 3, size // 32, 128), F32),
            pltpu.VMEM((3, size // 32, 128), F32),
            pltpu.VMEM((3, 3, size // 32, 128), F32),
            pltpu.VMEM((3, size // 2, 128), F32),
            pltpu.VMEM((5, 2, NBLK, width, BLOCK), BF16),
            pltpu.VMEM((3, 8, 128), F32),
            dma((parts,)), dma((parts,)), dma, dma((parts,)), dma((parts,)),
        ]
        + [dma((3, 3))] * 6 + [dma, dma, dma((3,)), dma((3,))]
        + [dma((3, 3))] * 10 + [dma, dma, dma((6,)), dma((6,))],
        compiler_params=pltpu.CompilerParams(collective_id=1, has_side_effects=True, vmem_limit_bytes=62 << 20),
        name="gather",
    )(grads, lat, ids, offsets, scales, momentum)


def back_kernel(final_ref, head_ref, mom_ref, scale_ref, newmom_ref, step_ref, high_ref, low_ref):
    new_momentum = MOMENTUM_DECAY * mom_ref[...] + head_ref[...]
    newmom_ref[...] = new_momentum
    high_ref[...], low_ref[...] = split(head_ref[...] + MOMENTUM_DECAY * new_momentum)
    width = CHUNK // 128
    for i in range(NBLK):
        rows = slice(i * BLOCK, (i + 1) * BLOCK)
        total = None
        for k in range(NBLK):
            ks = slice(k * BLOCK, (k + 1) * BLOCK)
            mh, ml = final_ref[0, k, rows, :], final_ref[1, k, rows, :]
            term = mxu(mh, high_ref[ks, :]) + mxu(mh, low_ref[ks, :]) + mxu(ml, high_ref[ks, :])
            total = term if total is None else total + term
        for at in range(width):
            lanes = slice(at * 128, (at + 1) * 128)
            step_ref[rows, lanes] = total[:, lanes] * scale_ref[pl.ds(pl.program_id(0) * width + at, 1), :]


def back(final, head, momentum, scale):
    width, count = head.shape
    return pl.pallas_call(
        back_kernel,
        grid=(count // CHUNK,),
        in_specs=[
            pl.BlockSpec(final.shape, lambda c: (0, 0, 0, 0)),
            pl.BlockSpec((width, CHUNK), lambda c: (0, c)),
            pl.BlockSpec((width, CHUNK), lambda c: (0, c)),
            pl.BlockSpec(scale.shape, lambda c: (0, 0)),
        ],
        out_specs=[pl.BlockSpec((width, CHUNK), lambda c: (0, c))] * 2,
        out_shape=[jax.ShapeDtypeStruct((width, count), F32)] * 2,
        scratch_shapes=[pltpu.VMEM((width, CHUNK), BF16), pltpu.VMEM((width, CHUNK), BF16)],
        compiler_params=pltpu.CompilerParams(vmem_limit_bytes=60 << 20),
        name="back",
    )(final, head, momentum, scale)


def per_device(factor_grads, latents, task_ids, offsets, target_scale, momentum):
    final, head, column_scale = gather(factor_grads, latents, task_ids, offsets, target_scale, momentum)
    new_momentum, step = back(final, head, momentum, column_scale)
    return new_momentum, step


def solution(mesh):
    placed = (
        P(("gx", "gy"), None),
        P(("gx", "gy"), None),
        P(("gx", "gy")),
        P(),
        P(),
        P(None, ("gx", "gy")),
    )
    return jax.shard_map(
        per_device,
        mesh=mesh,
        in_specs=placed,
        out_specs=(P(None, ("gx", "gy")), P(None, ("gx", "gy"))),
        check_vma=False,
    )
```

time: 129 us -> 117 us (0.907)
  Pallas kernels: 128 us -> 116 us
    pallas_call x1, Pallas kernels: 48.8 us -> 15.8 us  [back(): pl.pallas_call(back_kernel, grid=(count // CHUNK,), in_specs=[pl.BlockSpe...]
    pallas_call x1, Pallas kernels: 79.7 us -> 100 us  [gather(): pl.pallas_call(gather_kernel, in_specs=[anywhere, vmem, smem, smem, smem,...]
where the time goes in v4:
time: 117 us
  Pallas kernels  116 us (99%)
    pallas_call x1, Pallas kernels, gather(): pl.pallas_call(gather_kernel, in_specs=[anywhere, vmem, smem, smem, smem,...  100 us
    pallas_call x1, Pallas kernels, back(): pl.pallas_call(back_kernel, grid=(count // CHUNK,), in_specs=[pl.BlockSpe...  15.8 us

profile of v4, /device:TPU:1, one launch (start us, length us, event | category | flops | bytes accessed | tf_op | source)
XLA Modules:
  0.0 116.8 jit_solution(17778734429918157139)
XLA Ops:
  0.6 100.4 %gather.1 = (bf16[2,4,1024,256]{3,2,1,0:T(8,128)(2,1)}, f32[1024,1536]{1,0:T(8,128)}, f32[12,128]{1,0:T(8,128)}) custom-call(bf16[4,196608]{1,0:T(4,128)(2,1)} %grads_ref.1, bf16[4,1024]{1,0:T(4,128)(2,1)} %lat_ref.1, s32[4]{0:T(128)} %ids_ref.1, s32[160]{0:T(256)} %offsets_ref.1, f32[160]{0:T(256)} %scales_ref.1, f32[1024,1536]{1,0:T(8,128)} %mom_ref.3), custom_call_target="tpu_custom_call" | custom-call | tf_op jit(solution)/shard_map/gather/pallas_call | solution.py:432
  101.0 15.8 %back.1 = (f32[1024,1536]{1,0:T(8,128)}, f32[1024,1536]{1,0:T(8,128)}) custom-call(bf16[2,4,1024,256]{3,2,1,0:T(8,128)(2,1)} %get-tuple-element.5.final_ref, f32[1024,1536]{1,0:T(8,128)} %get-tuple-element.6.head_ref, f32[1024,1536]{1,0:T(8,128)} %mom_ref.3, f32[12,128]{1,0:T(8,128)} %get-tuple-element.7.scale_ref), custom_call_target="tpu_custom_call" | custom-call | tf_op jit(solution)/shard_map/back/pallas_call | solution.py:491

commit v5 on v4

--- a/solution.py
+++ b/solution.py
@@ -58,9 +58,11 @@
 
 
 def pair_of(slot):
-    row = lax.rem(slot, NBLK)
-    col = lax.rem(row + lax.div(slot, NBLK), NBLK)
-    return row, col
+    side = lax.div(slot - NBLK, 3)
+    turn = slot - NBLK - 3 * side
+    row = 2 * side + lax.div(turn, 2)
+    col = jnp.where(turn == 0, 2 * side + 1, jnp.where(turn == 1, 2 - side, 3 - 3 * side))
+    return jnp.where(slot < NBLK, slot, row), jnp.where(slot < NBLK, slot, col)
 
 
 def gather_kernel(grads_ref, lat_ref, ids_ref, offsets_ref, scales_ref, mom_ref,
@@ -251,20 +253,24 @@
         tuple((6, q) for q in every) + tuple((5, q) for q in every[2:])
         + tuple((9, q) for q in every) + tuple((8, q) for q in every[2:]),
     )
+    phase = []
+
+    def scatter(r):
+        cored[r].wait_recv()
+        half_ref[r] = packed_ref[r, span(core, halfs), :] + core_ref[r]
+        phase.append([
+            remote(half_ref.at[r, span(lax.rem(coord[r] + k, 4), quart)], got1_ref.at[r, k - 1],
+                   s1.at[r, k - 1], r1.at[r, k - 1], peer_of(where, r, k)) for k in hops])
+
     for r in range(3):
         for low, high in groups[r]:
             gram(widths[-1], low, high)
         for at, (slot, (i, j)) in enumerate(layout[r]):
             packed_ref[r, at * small : (at + 1) * small, :] = acc_ref[slot, i * small : (i + 1) * small, j * small : (j + 1) * small]
         cored.append(remote(packed_ref.at[r, span(other, halfs)], core_ref.at[r], cs.at[r], cr.at[r], peer_of(where, 3, 1)))
-
-    phase = []
-    for r in range(3):
-        cored[r].wait_recv()
-        half_ref[r] = packed_ref[r, span(core, halfs), :] + core_ref[r]
-        phase.append([
-            remote(half_ref.at[r, span(lax.rem(coord[r] + k, 4), quart)], got1_ref.at[r, k - 1],
-                   s1.at[r, k - 1], r1.at[r, k - 1], peer_of(where, r, k)) for k in hops])
+        if r:
+            scatter(r - 1)
+    scatter(2)
     phase2 = []
     for r in range(3):
         b = (r + 1) % 3
@@ -305,29 +311,41 @@
             return final_ref.at[part, col, rows_at, :]
         return mats_ref.at[which, part, col, rows_at, :]
 
-    def store(which, row, col, value, mirrored):
-        values = list(split(value))
-        tiles = [tile(which, 0, row, col), tile(which, 1, row, col)]
-        if mirrored:
-            values += list(split(value.T))
-            tiles += [tile(which, 0, col, row), tile(which, 1, col, row)]
-        for at, block in zip(tiles, values):
-            at[...] = block
-        for at in tiles:
-            pltpu.make_async_remote_copy(
-                src_ref=at, dst_ref=at, send_sem=ps.at[which], recv_sem=pr.at[which],
-                device_id=partner, device_id_type=MESH).start()
+    mine_a, mine_b = 2 * core, 2 * core + 1
+    far_e, far_f = 2 - core, 3 - 3 * core
+    corner_a, corner_b = (mine_a, mine_a), (mine_b, mine_b)
+    joint, cross_a, cross_b = (mine_a, mine_b), (mine_a, far_e), (mine_b, far_f)
+
+    def put(which, row, col, value):
+        for part, half_value in enumerate(split(value)):
+            tile(which, part, row, col)[...] = half_value
+
+    def push(which, *spots):
+        for row, col in spots:
+            for part in range(2):
+                at = tile(which, part, row, col)
+                pltpu.make_async_remote_copy(
+                    src_ref=at, dst_ref=at, send_sem=ps.at[which], recv_sem=pr.at[which],
+                    device_id=partner, device_id_type=MESH).start()
+
+    def store(which, spot, value):
+        row, col = spot
+        put(which, row, col, value)
+        if spot is corner_a or spot is corner_b:
+            return lambda: push(which, spot)
+        put(which, col, row, value.T)
+        if which == final:
+            return lambda: push(which, spot, (col, row))
+        if spot is joint:
+            return lambda: push(which, (1 + core, 3 * core))
+        return lambda: push(which, (col, row))
+
+    def tiles_of(which):
+        return mats_ref.at[0, 0] if which == final else mats_ref.at[0, 0, :, : 5 * BLOCK // 2, :]
 
     def finished(which):
-        one = final_ref.at[0] if which == final else mats_ref.at[which, 0]
+        one = tiles_of(which)
         pltpu.make_async_copy(one, one, pr.at[which]).wait()
-
-    def diagonal(t):
-        slot = 2 * core + t
-        return slot, slot
-
-    def beside(t):
-        return pair_of(4 + 3 * core + t)
 
     def block(r, at):
         return sums_ref[r, at * small : (at + 1) * small, :]
@@ -343,48 +361,49 @@
     squares = jnp.sum(jnp.sum(squares, axis=1, keepdims=True), axis=0, keepdims=True)
     trace_ref[0] = jnp.broadcast_to(squares, trace_ref.shape[1:])
     traced = remote(trace_ref.at[0], trace_ref.at[1], ts, tr, partner)
-    for t in range(2):
-        value = square([block(0, 3 * t), block(0, 3 * t + 1), block(0, 3 * t + 1).T, block(0, 3 * t + 2)])
-        store(G, *diagonal(t), value, False)
+    for t, spot in enumerate((corner_a, corner_b)):
+        store(G, spot, square([block(0, 3 * t), block(0, 3 * t + 1), block(0, 3 * t + 1).T, block(0, 3 * t + 2)]))()
     arrived(phase5[1])
-    store(G, *beside(0), square([block(1, at) for at in range(4)]), True)
+    store(G, joint, square([block(1, at) for at in range(4)]))()
     arrived(phase5[2])
-    store(G, *beside(1), square([block(1, 4), block(1, 5), block(2, 4), block(2, 5)]), True)
-    store(G, *beside(2), square([block(2, at) for at in range(4)]), True)
+    store(G, cross_a, square([block(1, 4), block(1, 5), block(2, 4), block(2, 5)]))()
+    store(G, cross_b, square([block(2, at) for at in range(4)]))()
     arrived([traced])
     inverse = 1.0 / (jnp.sqrt(trace_ref[0, 0:1, 0:1] + trace_ref[1, 0:1, 0:1]) + EPSILON)
     trace_ref[2] = jnp.broadcast_to(inverse, trace_ref.shape[1:])
     scale_ref[...] = scale_ref[...] * (math.sqrt(OUT) * inverse)
-    finished(G)
 
     def eye(row, col):
         i = lax.broadcasted_iota(jnp.int32, (BLOCK, BLOCK), 0)
         j = lax.broadcasted_iota(jnp.int32, (BLOCK, BLOCK), 1)
         return jnp.where((i == j) & (row == col), 1.0, 0.0)
 
-    def product(left, right, row, col):
-        total_block = None
-        for k in range(NBLK):
-            lh, ll = tile(left, 0, row, k)[...], tile(left, 1, row, k)[...]
-            rh, rl = tile(right, 0, k, col)[...], tile(right, 1, k, col)[...]
-            term = mxu(lh, rh) + mxu(lh, rl) + mxu(ll, rh)
-            total_block = term if total_block is None else total_block + term
-        return total_block
-
-    def stage(left, right, dest, finish):
-        def off(t, carry):
-            row, col = beside(t)
-            store(dest, row, col, finish(row, col, product(left, right, row, col)), True)
-            return carry
-
-        def on(t, carry):
-            row, col = diagonal(t)
-            store(dest, row, col, finish(row, col, product(left, right, row, col)), False)
-            return carry
-
-        lax.fori_loop(0, 3, off, 0)
-        lax.fori_loop(0, 2, on, 0)
-        finished(dest)
+    def triple(left, right, at, other_at, flip):
+        dot = mxu_t if flip else mxu
+        lh, ll = tile(left, 0, *at)[...], tile(left, 1, *at)[...]
+        rh, rl = tile(right, 0, *other_at)[...], tile(right, 1, *other_at)[...]
+        return dot(lh, rh) + dot(lh, rl) + dot(ll, rh)
+
+    def rows_of(left, right, row, col, ks):
+        return sum(triple(left, right, (row, k), (col, k), True) for k in ks)
+
+    def stage(left, right, dest, finish, latest):
+        value_a = rows_of(left, right, mine_a, mine_a, (mine_a, mine_b, far_e))
+        value_b = rows_of(left, right, mine_b, mine_b, (mine_a, mine_b, far_f))
+        value_j = rows_of(left, right, mine_a, mine_b, (mine_a, mine_b))
+        finished(latest)
+        value_a += rows_of(left, right, mine_a, mine_a, (far_f,))
+        value_b += rows_of(left, right, mine_b, mine_b, (far_e,))
+        pushes = [store(dest, corner_a, finish(*corner_a, value_a)), store(dest, corner_b, finish(*corner_b, value_b))]
+        value_j += rows_of(left, right, mine_a, mine_b, (far_e, far_f))
+        for go in pushes:
+            go()
+        value = sum(triple(left, right, (mine_a, k), (k, far_e), False) for k in (mine_a, mine_b, far_e))
+        value += triple(left, right, (mine_a, far_f), (far_e, far_f), True)
+        store(dest, joint, finish(*joint, value_j))()
+        value_b = sum(triple(left, right, (mine_b, k), (k, far_f), False) for k in (mine_a, mine_b, far_e, far_f))
+        store(dest, cross_a, finish(*cross_a, value))()
+        store(dest, cross_b, finish(*cross_b, value_b))()
 
     def newton(which, scaled):
         def finish(row, col, value):
@@ -402,15 +421,16 @@
         return (value * inv) * inv
 
     plain = lambda row, col, value: value
-    stage(G, G, M1, newton(G, True))
-    stage(G, M1, T, normal)
-    stage(T, M1, G2, plain)
-    stage(G2, G2, M2, newton(G2, False))
-    stage(M2, M1, final, plain)
+    stage(G, G, M1, newton(G, True), G)
+    stage(G, M1, T, normal, M1)
+    stage(T, M1, G2, plain, T)
+    stage(G2, G2, M2, newton(G2, False), G2)
+    stage(M2, M1, final, plain, M2)
+    finished(final)
     for copy in started:
         copy.wait_send()
     for which in range(6):
-        one = mats_ref.at[0, 0]
+        one = tiles_of(which)
         pltpu.make_async_copy(one, one, ps.at[which]).wait()
     for q in range(parts):
         sent = cols_refs[q].at[pl.ds(0, total - 1)]

time: 117 us -> 113 us (0.966)
  Pallas kernels: 116 us -> 112 us
    pallas_call x1, Pallas kernels: 100 us -> 96.7 us  [gather(): pl.pallas_call(gather_kernel, in_specs=[anywhere, vmem, smem, smem, smem,...]
where the time goes in v5:
time: 113 us
  Pallas kernels  112 us (99%)
    pallas_call x1, Pallas kernels, gather(): pl.pallas_call(gather_kernel, in_specs=[anywhere, vmem, smem, smem, smem,...  96.7 us
    pallas_call x1, Pallas kernels, back(): pl.pallas_call(back_kernel, grid=(count // CHUNK,), in_specs=[pl.BlockSpe...  15.6 us

profile of v5, /device:TPU:1, one launch (start us, length us, event | category | flops | bytes accessed | tf_op | source)
XLA Modules:
  0.0 113.0 jit_solution(4138130871314652367)
XLA Ops:
  0.6 96.7 %gather.1 = (bf16[2,4,1024,256]{3,2,1,0:T(8,128)(2,1)}, f32[1024,1536]{1,0:T(8,128)}, f32[12,128]{1,0:T(8,128)}) custom-call(bf16[4,196608]{1,0:T(4,128)(2,1)} %grads_ref.1, bf16[4,1024]{1,0:T(4,128)(2,1)} %lat_ref.1, s32[4]{0:T(128)} %ids_ref.1, s32[160]{0:T(256)} %offsets_ref.1, f32[160]{0:T(256)} %scales_ref.1, f32[1024,1536]{1,0:T(8,128)} %mom_ref.3), custom_call_target="tpu_custom_call" | custom-call | tf_op jit(solution)/shard_map/gather/pallas_call | solution.py:452
  97.4 15.6 %back.1 = (f32[1024,1536]{1,0:T(8,128)}, f32[1024,1536]{1,0:T(8,128)}) custom-call(bf16[2,4,1024,256]{3,2,1,0:T(8,128)(2,1)} %get-tuple-element.5.final_ref, f32[1024,1536]{1,0:T(8,128)} %get-tuple-element.6.head_ref, f32[1024,1536]{1,0:T(8,128)} %mom_ref.3, f32[12,128]{1,0:T(8,128)} %get-tuple-element.7.scale_ref), custom_call_target="tpu_custom_call" | custom-call | tf_op jit(solution)/shard_map/back/pallas_call | solution.py:511

commit v6 on v5

--- a/solution.py
+++ b/solution.py
@@ -89,12 +89,23 @@
     def device(to):
         return (lax.div(to, 8), lax.rem(to, 8))
 
-    def greet(k, carry):
-        to = lax.rem(me + lax.rem(k * 37, total), total)
+    def several(low, high, one):
+        groups = (high - low) // 4
+
+        def body(i, carry):
+            for j in range(4):
+                one(low + 4 * i + j)
+            return carry
+
+        lax.fori_loop(0, groups, body, 0)
+        for k in range(low + 4 * groups, high):
+            one(k)
+
+    def greet(k):
+        to = lax.rem(me + k * 37, total)
         pl.semaphore_signal(barrier, inc=1, device_id=device(to), device_id_type=MESH)
-        return carry
-
-    lax.fori_loop(1, total, greet, 0)
+
+    several(1, total, greet)
 
     loads = []
     for q in range(parts):
@@ -164,14 +175,13 @@
         pltpu.make_async_copy(columns_of(me, q), cols_refs[q].at[me], gr.at[q]).start()
 
     def send(q, low, high):
-        def body(k, carry):
-            to = lax.rem(me + lax.rem(k * 37, total), total)
+        def one(k):
+            to = lax.rem(me + k * 37, total)
             pltpu.make_async_remote_copy(
                 src_ref=columns_of(to, q), dst_ref=cols_refs[q].at[me], send_sem=gs.at[q], recv_sem=gr.at[q],
                 device_id=device(to), device_id_type=MESH).start()
-            return carry
-
-        lax.fori_loop(low, high, body, 0)
+
+        several(low, high, one)
 
     send(0, 1, 48)
     keep.wait()
@@ -454,7 +464,7 @@
         in_specs=[anywhere, vmem, smem, smem, smem, anywhere],
         out_specs=[vmem, anywhere, vmem],
         out_shape=[
-            jax.ShapeDtypeStruct((2, NBLK, width, BLOCK), BF16),
+            pltpu.VMEM((2, NBLK, width, BLOCK), BF16),
             jax.ShapeDtypeStruct((width, count), F32),
             jax.ShapeDtypeStruct((count // 128, 128), F32),
         ],
@@ -483,7 +493,7 @@
         ]
         + [dma((3, 3))] * 6 + [dma, dma, dma((3,)), dma((3,))]
         + [dma((3, 3))] * 10 + [dma, dma, dma((6,)), dma((6,))],
-        compiler_params=pltpu.CompilerParams(collective_id=1, has_side_effects=True, vmem_limit_bytes=62 << 20),
+        compiler_params=pltpu.CompilerParams(collective_id=1, has_side_effects=True, vmem_limit_bytes=58 << 20),
         name="gather",
     )(grads, lat, ids, offsets, scales, momentum)
 
@@ -512,7 +522,7 @@
         back_kernel,
         grid=(count // CHUNK,),
         in_specs=[
-            pl.BlockSpec(final.shape, lambda c: (0, 0, 0, 0)),
+            pl.BlockSpec(memory_space=pltpu.VMEM),
             pl.BlockSpec((width, CHUNK), lambda c: (0, c)),
             pl.BlockSpec((width, CHUNK), lambda c: (0, c)),
             pl.BlockSpec(scale.shape, lambda c: (0, 0)),
@@ -520,7 +530,7 @@
         out_specs=[pl.BlockSpec((width, CHUNK), lambda c: (0, c))] * 2,
         out_shape=[jax.ShapeDtypeStruct((width, count), F32)] * 2,
         scratch_shapes=[pltpu.VMEM((width, CHUNK), BF16), pltpu.VMEM((width, CHUNK), BF16)],
-        compiler_params=pltpu.CompilerParams(vmem_limit_bytes=60 << 20),
+        compiler_params=pltpu.CompilerParams(vmem_limit_bytes=48 << 20),
         name="back",
     )(final, head, momentum, scale)
 

time: 113 us -> 110 us (0.973)
  Pallas kernels: 112 us -> 109 us
    pallas_call x1, Pallas kernels: 96.7 us -> 94.3 us  [gather(): pl.pallas_call(gather_kernel, in_specs=[anywhere, vmem, smem, smem, smem,...]
where the time goes in v6:
time: 110 us
  Pallas kernels  109 us (99%)
    pallas_call x1, Pallas kernels, gather(): pl.pallas_call(gather_kernel, in_specs=[anywhere, vmem, smem, smem, smem,...  94.3 us
    pallas_call x1, Pallas kernels, back(): pl.pallas_call(back_kernel, grid=(count // CHUNK,), in_specs=[pl.BlockSpe...  14.6 us

profile of v6, /device:TPU:1, one launch (start us, length us, event | category | flops | bytes accessed | tf_op | source)
XLA Modules:
  0.0 110.3 jit_solution(16035276758861474287)
XLA Ops:
  0.6 94.3 %gather.1 = (bf16[2,4,1024,256]{3,2,1,0:T(8,128)(2,1)S(1)}, f32[1024,1536]{1,0:T(8,128)}, f32[12,128]{1,0:T(8,128)}) custom-call(bf16[4,196608]{1,0:T(4,128)(2,1)} %grads_ref.1, bf16[4,1024]{1,0:T(4,128)(2,1)} %lat_ref.1, s32[4]{0:T(128)} %ids_ref.1, s32[160]{0:T(256)} %offsets_ref.1, f32[160]{0:T(256)} %scales_ref.1, f32[1024,1536]{1,0:T(8,128)} %mom_ref.3), custom_call_target="tpu_custom_call" | custom-call | tf_op jit(solution)/shard_map/gather/pallas_call | solution.py:462
  94.9 0.0 copy-start
  94.9 0.7 copy-done
  95.6 14.6 %back.1 = (f32[1024,1536]{1,0:T(8,128)}, f32[1024,1536]{1,0:T(8,128)}) custom-call(bf16[2,4,1024,256]{3,2,1,0:T(8,128)(2,1)S(1)} %get-tuple-element.5.final_ref, f32[1024,1536]{1,0:T(8,128)} %get-tuple-element.6.head_ref, f32[1024,1536]{1,0:T(8,128)} %mom_ref.3, f32[12,128]{1,0:T(8,128)S(1)} %copy-done), custom_call_target="tpu_custom_call" | custom-call | tf_op jit(solution)/shard_map/back/pallas_call | solution.py:521
Async XLA Ops:
  94.9 0.7 copy-start
